TPU v7x, 768 devices: a whole 4x8x12 slice. The times are simulated.
768 devices in a mesh: dp: 32 (over y, x), row: 6 (over z_lo, core), col: 4 (over z_hi).
Axes of the slice: x: 4, y: 8, z: 12 (z_hi: 4, z_lo: 3; z = z_hi * 3 + z_lo), core: 2. Of those that a mesh axis runs over, the one named last changes fastest.
Arguments:
- attn_heads: bfloat16 [98304, 2304], P(('dp', 'col'), 'row'), may hold values from -6 to 6
- out_weight: bfloat16 [2304, 4096], P('row', 'col'), may hold values from -0.125 to 0.125
- cotangent: bfloat16 [98304, 4096], P(('dp', 'row'), 'col'), may hold values from -6 to 6
Outputs:
- head_grad: bfloat16 [98304, 2304], P(('dp', 'col'), 'row')
- weight_grad: float32 [2304, 4096], P('row', 'col')
All inputs are finite; a program needn't handle non-finite values.
Results may differ from a plain program's by a relative error of at most 0.015.
Values may be sent and summed in bfloat16 or wider, within the bound.
No kernel may reach another device: no remote copies, remote signals or barrier semaphores. Data moves between devices by JAX's collectives and lax.ppermute only.
A program may use at most 32 MiB of HBM per device.

v0:
```python
import jax
import jax.numpy as jnp
from jax import lax
from jax.experimental import pallas as pl
from jax.experimental.pallas import tpu as pltpu
from jax.sharding import Mesh, PartitionSpec as P


Y, X, ZL, CORE, ZH = 8, 4, 3, 2, 4
ROW = ZL * CORE
CHUNKS = 2
LANE = 128
XS = 4


SMEM = pl.BlockSpec(memory_space=pltpu.SMEM)
VMEM = pl.BlockSpec(memory_space=pltpu.VMEM)


def ring(n, step):
    return [(i, (i + step) % n) for i in range(n)]


def spread_pairs(k):
    pairs = []
    for row in range(ROW):
        for col in range(ZH):
            d = ZH * row + (col + k) % ZH
            pairs.append((row * ZH + col, (d % ROW) * ZH + d // ROW))
    return pairs


def gather_tokens(got, at):
    blk, feat = got[0].shape
    n = feat // CHUNKS

    def kernel(at_ref, *refs):
        outs = refs[ZH:]
        for col in range(ZH):
            k = (at_ref[0] + (ZH - col)) % ZH
            for i in range(ZH):

                @pl.when(k == i)
                def _():
                    for h in range(CHUNKS):
                        for s in range(XS):
                            fro = h * n + s * LANE
                            outs[h][s, :, col * LANE:(col + 1) * LANE] = refs[i][:, fro:fro + LANE]

    return pl.pallas_call(
        kernel,
        out_shape=[jax.ShapeDtypeStruct((XS, blk, ZH * LANE), got[0].dtype)] * CHUNKS,
        in_specs=[SMEM] + [VMEM] * ZH,
        out_specs=[VMEM] * CHUNKS,
        name="gather_tokens",
    )(at.reshape(1), *got)


def order_heads(pieces, rows, at):
    tok, hid = pieces[0].shape
    n = len(rows[0])
    blk = tok // ROW

    def kernel(at_ref, rows_ref, *refs):
        outs = refs[X:]
        for k in range(X):
            x = (at_ref[0] + (X - k)) % X
            for o, out in enumerate(outs):
                for i in range(n):
                    fro = pl.multiple_of(rows_ref[o * n + i] * blk, blk)
                    to = pl.multiple_of((i * X + x) * blk, blk)
                    out[:, pl.ds(to, blk)] = refs[k][pl.ds(fro, blk), :].T

    return pl.pallas_call(
        kernel,
        out_shape=[jax.ShapeDtypeStruct((hid, n * X * blk), pieces[0].dtype)] * len(rows),
        in_specs=[SMEM, SMEM] + [VMEM] * X,
        out_specs=[VMEM] * len(rows),
        name="order_heads",
    )(at.reshape(1), jnp.stack([r for group in rows for r in group]), *pieces)


def spread_cols(pieces, at):
    shape = pieces[0].shape

    def kernel(at_ref, *refs):
        out = refs[-1]
        for col in range(ZH):
            k = (at_ref[0] + (ZH - col)) % ZH
            for i in range(ZH):

                @pl.when(k == i)
                def _():
                    v = refs[i][...]
                    for y in range(Y):
                        out[y, col] = v

    return pl.pallas_call(
        kernel,
        out_shape=jax.ShapeDtypeStruct((Y, ZH) + shape, pieces[0].dtype),
        in_specs=[SMEM] + [VMEM] * ZH,
        out_specs=VMEM,
        name="spread_cols",
    )(at.reshape(1), *pieces)


def weight_rows(pieces):
    _, _, rows, wc = pieces.shape

    def kernel(src, out):
        for y in range(Y):
            for col in range(ZH):
                for s in range(wc // LANE):
                    to = (s * ZH + col) * LANE
                    out[y * rows:(y + 1) * rows, to:to + LANE] = src[y, col, :, s * LANE:(s + 1) * LANE]

    return pl.pallas_call(
        kernel,
        out_shape=jax.ShapeDtypeStruct((Y * rows, ZH * wc), pieces.dtype),
        in_specs=[VMEM],
        out_specs=VMEM,
        name="weight_rows",
    )(pieces)


def weight_part(heads_t, own, oth):
    hid = heads_t[0].shape[0]
    rows = hid // Y

    def kernel(a, b, c, d, out):
        acc = jnp.dot(a[...], c[...], preferred_element_type=jnp.float32)
        acc += jnp.dot(b[...], d[...], preferred_element_type=jnp.float32)
        acc = acc.astype(out.dtype)
        for y in range(Y):
            for col in range(ZH):
                out[y, col] = acc[y * rows:(y + 1) * rows, col * LANE:(col + 1) * LANE]

    return pl.pallas_call(
        kernel,
        out_shape=jax.ShapeDtypeStruct((Y, ZH, rows, LANE), own.dtype),
        in_specs=[VMEM] * 4,
        out_specs=VMEM,
        name="weight_part",
    )(*heads_t, own, oth)


def heads_part(owns, oths, weight, rows, at):
    hid, feat = weight.shape
    n = feat // CHUNKS
    count = len(rows[0])
    blk = owns[0].shape[0] // (count * X)

    def kernel(at_ref, rows_ref, *refs):
        sides = (refs[:CHUNKS], refs[CHUNKS:2 * CHUNKS])
        w_ref, outs = refs[2 * CHUNKS], refs[2 * CHUNKS + 1:]
        for k in range(X):
            x = (at_ref[0] + k) % X
            for o, side in enumerate(sides):
                for i in range(count):
                    fro = pl.multiple_of((i * X + x) * blk, blk)
                    acc = None
                    for h in range(CHUNKS):
                        prod = lax.dot_general(
                            side[h][pl.ds(fro, blk), :], w_ref[:, h * n:(h + 1) * n], (((1,), (1,)), ((), ())),
                            preferred_element_type=jnp.float32,
                        )
                        acc = prod if acc is None else acc + prod
                    to = pl.multiple_of(rows_ref[o * count + i] * blk, blk)
                    outs[k][pl.ds(to, blk), :] = acc.astype(weight.dtype)

    return pl.pallas_call(
        kernel,
        out_shape=[jax.ShapeDtypeStruct((2 * count * blk, hid), weight.dtype)] * X,
        in_specs=[SMEM, SMEM] + [VMEM] * (2 * CHUNKS + 1),
        out_specs=[VMEM] * X,
        name="heads_part",
    )(at.reshape(1), jnp.stack([r for group in rows for r in group]), *owns, *oths, weight)


def heads_sum(parts):
    def kernel(*refs):
        total = None
        for ref in refs[:-1]:
            v = ref[...].astype(jnp.float32)
            total = v if total is None else total + v
        refs[-1][...] = total.astype(refs[-1].dtype)

    tok, hid = parts[0].shape
    spec = pl.BlockSpec((tok // 4, hid), lambda i: (i, 0))
    return pl.pallas_call(
        kernel,
        grid=(4,),
        out_shape=jax.ShapeDtypeStruct((tok, hid), parts[0].dtype),
        in_specs=[spec] * len(parts),
        out_specs=spec,
        name="heads_sum",
    )(*parts)


def sum_rows(parts):
    _, _, rows, _ = parts[0].shape

    def kernel(*refs):
        out = refs[-1]
        for h in range(CHUNKS):
            for col in range(ZH):
                out[col, h] = jnp.sum(refs[h][:, col].astype(jnp.float32), axis=0).astype(out.dtype)

    return pl.pallas_call(
        kernel,
        out_shape=jax.ShapeDtypeStruct((ZH, CHUNKS, rows, LANE), parts[0].dtype),
        in_specs=[VMEM] * CHUNKS,
        out_specs=VMEM,
        name="sum_rows",
    )(*parts)


def spread_sum(parts):
    shape = (Y,) + parts.shape[1:]

    def kernel(src, out):
        total = jnp.sum(src[...].astype(jnp.float32), axis=0).astype(out.dtype)
        for y in range(Y):
            out[y] = total

    return pl.pallas_call(
        kernel,
        out_shape=jax.ShapeDtypeStruct(shape, parts.dtype),
        in_specs=[VMEM],
        out_specs=VMEM,
        name="spread_sum",
    )(parts)


def spread_rows(parts):
    rows = parts.shape[2]

    def kernel(src, out):
        for x in range(X):
            for y in range(Y):
                for h in range(CHUNKS):
                    out[x, h, y * rows:(y + 1) * rows] = src[y, h]

    return pl.pallas_call(
        kernel,
        out_shape=jax.ShapeDtypeStruct((X, CHUNKS, Y * rows, LANE), parts.dtype),
        in_specs=[VMEM],
        out_specs=VMEM,
        name="spread_rows",
    )(parts)


def finish(parts, scale):
    hid = parts.shape[2]
    rows = hid // 2

    def kernel(src, out):
        for h in range(CHUNKS):
            for x in range(X):
                at = (h * X + x) * LANE
                out[:, at:at + LANE] = src[x, h].astype(jnp.float32) * scale

    return pl.pallas_call(
        kernel,
        grid=(2,),
        out_shape=jax.ShapeDtypeStruct((hid, CHUNKS * X * LANE), jnp.float32),
        in_specs=[pl.BlockSpec((X, CHUNKS, rows, LANE), lambda i: (0, 0, i, 0))],
        out_specs=pl.BlockSpec((rows, CHUNKS * X * LANE), lambda i: (i, 0)),
        name="finish",
    )(parts)


def per_device(heads, weight, cot):
    xi, yi = lax.axis_index("x"), lax.axis_index("y")
    zl, core, zh = lax.axis_index("zl"), lax.axis_index("core"), lax.axis_index("zh")
    tok, feat = cot.shape
    hid = weight.shape[0]
    blk = tok // ZH
    grad_scale = float(heads.shape[0] * ZH * Y * X) ** (-0.5)

    def order(m, c):
        return (m % ZL) * CORE + c

    rows = [[order(zl, c), order(zl + 2, c), order(zl + 1, c)] for c in (core, 1 - core)]

    sends = [lax.dynamic_slice(cot, ((zh + k) % ZH * blk, 0), (blk, feat)) for k in range(ZH)]
    got = [lax.ppermute(sends[k], ("zl", "core", "zh"), spread_pairs(k)) for k in range(ZH)]

    heads_x = [heads] + [lax.ppermute(heads, "x", ring(X, k)) for k in range(1, X)]
    heads_t = order_heads(heads_x, rows, xi)

    mine = gather_tokens(got, (zh * ROW + zl * CORE + core) % ZH)
    near = []
    for h in range(CHUNKS):
        part = lax.all_to_all(mine[h], "x", 0, 0)
        part = part.reshape(X * blk, ZH * LANE)
        near.append([part] + [lax.ppermute(part, "zl", ring(ZL, k)) for k in (1, 2)])

    wr = hid // Y
    w_part = jnp.concatenate(
        [lax.dynamic_slice(weight, (yi * wr, (h * X + xi) * LANE), (wr, LANE)) for h in range(CHUNKS)], axis=1
    )
    w_far = [lax.ppermute(w_part, "zh", ring(ZH, k)) for k in range(1, ZH)]
    w_y = spread_cols([w_part] + w_far, zh)
    w_y = lax.all_to_all(w_y, "y", 0, 0)
    w_y = weight_rows(w_y)

    owns, oths, parts = [], [], []
    for h in range(CHUNKS):
        own = jnp.concatenate(near[h], axis=0)
        oth = lax.ppermute(own, "core", ring(CORE, 1))
        owns.append(own)
        oths.append(oth)
        part = weight_part(heads_t, own, oth)
        parts.append(lax.all_to_all(part, "y", 0, 0))
    r = sum_rows(parts)
    r = lax.all_to_all(r, "zh", 0, 0)
    r = spread_sum(r)
    r = lax.all_to_all(r, "y", 0, 0)
    r = spread_rows(r)
    r = lax.all_to_all(r, "x", 0, 0)
    weight_grad = finish(r, grad_scale)

    part = heads_part(owns, oths, w_y, rows, xi)
    part = [part[0]] + [lax.ppermute(part[k], "x", ring(X, k)) for k in range(1, X)]
    head_grad = heads_sum(part)
    return head_grad, weight_grad


def solution(mesh):
    fine = Mesh(mesh.devices.reshape(Y, X, ZL, CORE, ZH), ("y", "x", "zl", "core", "zh"))

    return jax.shard_map(
        per_device,
        mesh=fine,
        in_specs=(P(("y", "x", "zh"), ("zl", "core")), P(("zl", "core"), "zh"), P(("y", "x", "zl", "core"), "zh")),
        out_specs=(P(("y", "x", "zh"), ("zl", "core")), P(("zl", "core"), "zh")),
        check_vma=False,
    )
```

profile of v0, /device:TPU:78, one launch (start us, length us, event | category | flops | bytes accessed | tf_op | source)
XLA Modules:
  0.0 318.3 jit_solution(622340577794147604)
XLA Ops:
  2.0 10.4 %collective-permute-start.3 = (bf16[128,1024]{1,0:T(8,128)(2,1)S(1)}, bf16[128,1024]{1,0:T(8,128)(2,1)S(1)}, u32[]{:S(2)}, u32[]{:S(2)}) collective-permute-start(bf16[128,1024]{1,0:T(8,128)(2,1)S(1)} %get-tuple-element.18), channel_id=1, source_target_pairs={{0,12},{1,0},{2,4},{3,8},{4,5},{5,16},{6,20},{7,1},{8,21},{9,9},{1... | collective-permute-start | bytes 786440 | tf_op jit(solution)/shard_map/ppermute | solution.py:287
  16.9 5.2 %collective-permute-start = (bf16[128,1024]{1,0:T(8,128)(2,1)S(1)}, bf16[128,1024]{1,0:T(8,128)(2,1)S(1)}, u32[]{:S(2)}, u32[]{:S(2)}) collective-permute-start(bf16[128,1024]{1,0:T(8,128)(2,1)S(1)} %get-tuple-element.20), channel_id=1, source_target_pairs={{0,0},{1,4},{2,8},{3,12},{4,16},{5,20},{6,1},{7,5},{8,9},{9,13},{1... | collective-permute-start | bytes 786440 | tf_op jit(solution)/shard_map/ppermute | solution.py:287
  31.0 22.2 %collective-permute-done.refs_0_ = bf16[128,1024]{1,0:T(8,128)(2,1)S(1)} collective-permute-done((bf16[128,1024]{1,0:T(8,128)(2,1)S(1)}, bf16[128,1024]{1,0:T(8,128)(2,1)S(1)}, u32[]{:S(2)}, u32[]{:S(2)}) %collective-permute-start) | collective-permute-done | bytes 262176 | tf_op jit(solution)/shard_map/ppermute | solution.py:287
  56.4 12.6 %all_to_all.40 = bf16[4,128,512]{2,1,0:T(8,128)(2,1)S(1)} all-to-all(bf16[4,128,512]{2,1,0:T(8,128)(2,1)} %get-tuple-element.10), channel_id=1, replica_groups=mesh['y'=8,'x'=4,'zl'=3,'core'=2,'zh'=4] {'x'}, dimensions={0} | all-to-all | bytes 1048576 | tf_op jit(solution)/shard_map/all_to_all | solution.py:295
  74.9 11.9 %all_to_all.41 = bf16[4,128,512]{2,1,0:T(8,128)(2,1)S(1)} all-to-all(bf16[4,128,512]{2,1,0:T(8,128)(2,1)} %get-tuple-element.11), channel_id=1, replica_groups=mesh['y'=8,'x'=4,'zl'=3,'core'=2,'zh'=4] {'x'}, dimensions={0} | all-to-all | bytes 1048576 | tf_op jit(solution)/shard_map/all_to_all | solution.py:295
  98.9 9.3 %collective-permute-done.7 = bf16[512,512]{1,0:T(8,128)(2,1)S(1)} collective-permute-done((bf16[512,512]{1,0:T(8,128)(2,1)S(1)}, bf16[512,512]{1,0:T(8,128)(2,1)S(1)}, u32[]{:S(2)}, u32[]{:S(2)}) %collective-permute-start.7) | collective-permute-done | bytes 524320 | tf_op jit(solution)/shard_map/ppermute | solution.py:297
  108.2 8.9 %collective-permute-done.6 = bf16[512,512]{1,0:T(8,128)(2,1)S(1)} collective-permute-done((bf16[512,512]{1,0:T(8,128)(2,1)S(1)}, bf16[512,512]{1,0:T(8,128)(2,1)S(1)}, u32[]{:S(2)}, u32[]{:S(2)}) %collective-permute-start.6) | collective-permute-done | bytes 524320 | tf_op jit(solution)/shard_map/ppermute | solution.py:297
  129.7 9.4 %collective-permute-done.17.refs_2_ = bf16[768,384]{1,0:T(8,128)(2,1)} collective-permute-done((bf16[768,384]{1,0:T(8,128)(2,1)}, bf16[768,384]{1,0:T(8,128)(2,1)}, u32[]{:S(2)}, u32[]{:S(2)}) %collective-permute-start.17) | collective-permute-done | bytes 589856 | tf_op jit(solution)/shard_map/ppermute | solution.py:289
  139.1 11.6 %collective-permute-done.16.refs_1_ = bf16[768,384]{1,0:T(8,128)(2,1)} collective-permute-done((bf16[768,384]{1,0:T(8,128)(2,1)}, bf16[768,384]{1,0:T(8,128)(2,1)}, u32[]{:S(2)}, u32[]{:S(2)}) %collective-permute-start.16) | collective-permute-done | bytes 589856 | tf_op jit(solution)/shard_map/ppermute | solution.py:289
  159.6 7.5 %all-to-all-start.3 = ((bf16[8,4,48,128]{3,2,1,0:T(8,128)(2,1)}), bf16[8,4,48,128]{3,2,1,0:T(8,128)(2,1)S(1)}, u32[]{:S(2)}, u32[]{:S(2)}) async-start(bf16[8,4,48,128]{3,2,1,0:T(8,128)(2,1)} %weight_part.2), calls=%async_computation.3 | async-start | bytes 786432 | tf_op jit(solution)/shard_map/all_to_all | solution.py:315
  167.1 4.7 %weight_part.3 = bf16[8,4,48,128]{3,2,1,0:T(8,128)(2,1)} custom-call(bf16[384,1536]{1,0:T(8,128)(2,1)} %get-tuple-element.16.a, bf16[384,1536]{1,0:T(8,128)(2,1)} %get-tuple-element.17.b, bf16[1536,512]{1,0:T(8,128)(2,1)} %copy-done.1, bf16[1536,512]{1,0:T(8,128)(2,1)} %collective-permute-done.9.refs_3_.d), custom_call_target="tpu_custom_call" | custom-call | tf_op jit(solution)/shard_map/weight_part/pallas_call | solution.py:138
  171.9 8.7 %all-to-all-done.3.refs_0_ = bf16[8,4,48,128]{3,2,1,0:T(8,128)(2,1)S(1)} async-done(((bf16[8,4,48,128]{3,2,1,0:T(8,128)(2,1)}), bf16[8,4,48,128]{3,2,1,0:T(8,128)(2,1)S(1)}, u32[]{:S(2)}, u32[]{:S(2)}) %all-to-all-start.3) | async-done | bytes 393248 | tf_op jit(solution)/shard_map/all_to_all | solution.py:315
  180.6 4.8 %all-to-all-start.4 = ((bf16[8,4,48,128]{3,2,1,0:T(8,128)(2,1)}), bf16[8,4,48,128]{3,2,1,0:T(8,128)(2,1)S(1)}, u32[]{:S(2)}, u32[]{:S(2)}) async-start(bf16[8,4,48,128]{3,2,1,0:T(8,128)(2,1)} %weight_part.3), calls=%async_computation.4 | async-start | bytes 786432 | tf_op jit(solution)/shard_map/all_to_all | solution.py:315
  185.4 13.6 %all-to-all-done.4.refs_1_ = bf16[8,4,48,128]{3,2,1,0:T(8,128)(2,1)S(1)} async-done(((bf16[8,4,48,128]{3,2,1,0:T(8,128)(2,1)}), bf16[8,4,48,128]{3,2,1,0:T(8,128)(2,1)S(1)}, u32[]{:S(2)}, u32[]{:S(2)}) %all-to-all-start.4) | async-done | bytes 393248 | tf_op jit(solution)/shard_map/all_to_all | solution.py:315
  201.6 5.1 %all-to-all-start.5 = ((bf16[4,2,48,128]{3,2,1,0:T(8,128)(2,1)}), bf16[4,2,48,128]{3,2,1,0:T(8,128)(2,1)S(1)}, u32[]{:S(2)}, u32[]{:S(2)}) async-start(bf16[4,2,48,128]{3,2,1,0:T(8,128)(2,1)} %sum_rows.1), calls=%async_computation.5 | async-start | bytes 196608 | tf_op jit(solution)/shard_map/all_to_all | solution.py:317
  207.4 6.9 %collective-permute-start.12 = (bf16[48,256]{1,0:T(8,128)(2,1)S(1)}, bf16[48,256]{1,0:T(8,128)(2,1)S(1)}, u32[]{:S(2)}, u32[]{:S(2)}) collective-permute-start(bf16[48,256]{1,0:T(8,128)(2,1)S(1)} %pad_maximum_fusion.2.refs_0_), channel_id=1, source_target_pairs={{0,3},{1,0},{2,1},{3,2},{4,7},{5,4},{6,5},{7,6},{8,11},{9,8},{10,9... | collective-permute-start | bytes 73736 | tf_op jit(solution)/shard_map/ppermute | solution.py:303
  214.4 5.2 %collective-permute-start.11 = (bf16[48,256]{1,0:T(8,128)(2,1)S(1)}, bf16[48,256]{1,0:T(8,128)(2,1)S(1)}, u32[]{:S(2)}, u32[]{:S(2)}) collective-permute-start(bf16[48,256]{1,0:T(8,128)(2,1)S(1)} %pad_maximum_fusion.2.refs_0_), channel_id=1, source_target_pairs={{0,2},{1,3},{2,0},{3,1},{4,6},{5,7},{6,4},{7,5},{8,10},{9,11},{10,... | collective-permute-start | bytes 73736 | tf_op jit(solution)/shard_map/ppermute | solution.py:303
  219.6 7.5 %collective-permute-start.10 = (bf16[48,256]{1,0:T(8,128)(2,1)S(1)}, bf16[48,256]{1,0:T(8,128)(2,1)S(1)}, u32[]{:S(2)}, u32[]{:S(2)}) collective-permute-start(bf16[48,256]{1,0:T(8,128)(2,1)S(1)} %pad_maximum_fusion.2.refs_0_), channel_id=1, source_target_pairs={{0,1},{1,2},{2,3},{3,0},{4,5},{5,6},{6,7},{7,4},{8,9},{9,10},{10,1... | collective-permute-start | bytes 73736 | tf_op jit(solution)/shard_map/ppermute | solution.py:303
  231.1 4.9 %all-to-all-start.2 = ((bf16[8,4,48,256]{3,2,1,0:T(8,128)(2,1)}), bf16[8,4,48,256]{3,2,1,0:T(8,128)(2,1)S(1)}, u32[]{:S(2)}, u32[]{:S(2)}) async-start(bf16[8,4,48,256]{3,2,1,0:T(8,128)(2,1)} %spread_cols.1), calls=%async_computation.2 | async-start | bytes 1572864 | tf_op jit(solution)/shard_map/all_to_all | solution.py:305
  237.6 19.1 %all-to-all-done.2.src = bf16[8,4,48,256]{3,2,1,0:T(8,128)(2,1)S(1)} async-done(((bf16[8,4,48,256]{3,2,1,0:T(8,128)(2,1)}), bf16[8,4,48,256]{3,2,1,0:T(8,128)(2,1)S(1)}, u32[]{:S(2)}, u32[]{:S(2)}) %all-to-all-start.2) | async-done | bytes 786464 | tf_op jit(solution)/shard_map/all_to_all | solution.py:305
  263.6 9.4 %heads_part.1 = (bf16[768,384]{1,0:T(8,128)(2,1)}, bf16[768,384]{1,0:T(8,128)(2,1)}, bf16[768,384]{1,0:T(8,128)(2,1)}, bf16[768,384]{1,0:T(8,128)(2,1)}) custom-call(s32[1]{0:T(128)} %bitcast.at_ref, s32[6]{0:T(128)} %stack.34.rows_ref, bf16[1536,512]{1,0:T(8,128)(2,1)} %copy-done, bf16[1536,512]{1,0:T(8,128)(2,1)} %copy-done.1, ...), custom_call_target="tpu_custom_call" | custom-call | tf_op jit(solution)/shard_map/heads_part/pallas_call | solution.py:171
  284.9 6.1 %all-to-all-start.7 = ((bf16[4,2,384,128]{3,2,1,0:T(8,128)(2,1)}), bf16[4,2,384,128]{3,2,1,0:T(8,128)(2,1)S(1)}, u32[]{:S(2)}, u32[]{:S(2)}) async-start(bf16[4,2,384,128]{3,2,1,0:T(8,128)(2,1)} %spread_rows.1), calls=%async_computation.7 | async-start | bytes 1572864 | tf_op jit(solution)/shard_map/all_to_all | solution.py:321
  290.9 11.0 %collective-permute-done.13.refs_1_ = bf16[768,384]{1,0:T(8,128)(2,1)S(1)} collective-permute-done((bf16[768,384]{1,0:T(8,128)(2,1)}, bf16[768,384]{1,0:T(8,128)(2,1)S(1)}, u32[]{:S(2)}, u32[]{:S(2)}) %collective-permute-start.13) | collective-permute-done | bytes 589856 | tf_op jit(solution)/shard_map/ppermute | solution.py:325
  301.9 5.0 %collective-permute-done.15.refs_3_ = bf16[768,384]{1,0:T(8,128)(2,1)S(1)} collective-permute-done((bf16[768,384]{1,0:T(8,128)(2,1)}, bf16[768,384]{1,0:T(8,128)(2,1)S(1)}, u32[]{:S(2)}, u32[]{:S(2)}) %collective-permute-start.15) | collective-permute-done | bytes 589856 | tf_op jit(solution)/shard_map/ppermute | solution.py:325
  (84 shorter events, 96.2 us)
Async XLA Ops:
  2.0 25.7 %collective-permute-start.3 = (bf16[128,1024]{1,0:T(8,128)(2,1)S(1)}, bf16[128,1024]{1,0:T(8,128)(2,1)S(1)}, u32[]{:S(2)}, u32[]{:S(2)}) collective-permute-start(bf16[128,1024]{1,0:T(8,128)(2,1)S(1)} %get-tuple-element.18), channel_id=1, source_target_pairs={{0,12},{1,0},{2,4},{3,8},{4,5},{5,16},{6,20},{7,1},{8,21},{9,9},{1... | collective-permute-start | bytes 786440 | tf_op jit(solution)/shard_map/ppermute | solution.py:287
  12.3 18.7 %collective-permute-start.1 = (bf16[128,1024]{1,0:T(8,128)(2,1)S(1)}, bf16[128,1024]{1,0:T(8,128)(2,1)S(1)}, u32[]{:S(2)}, u32[]{:S(2)}) collective-permute-start(bf16[128,1024]{1,0:T(8,128)(2,1)S(1)} %get-tuple-element.19), channel_id=1, source_target_pairs={{0,4},{1,8},{2,12},{3,0},{4,20},{5,1},{6,5},{7,16},{8,13},{9,17},{... | collective-permute-start | bytes 786440 | tf_op jit(solution)/shard_map/ppermute | solution.py:287
  16.9 36.3 %collective-permute-start = (bf16[128,1024]{1,0:T(8,128)(2,1)S(1)}, bf16[128,1024]{1,0:T(8,128)(2,1)S(1)}, u32[]{:S(2)}, u32[]{:S(2)}) collective-permute-start(bf16[128,1024]{1,0:T(8,128)(2,1)S(1)} %get-tuple-element.20), channel_id=1, source_target_pairs={{0,0},{1,4},{2,8},{3,12},{4,16},{5,20},{6,1},{7,5},{8,9},{9,13},{1... | collective-permute-start | bytes 786440 | tf_op jit(solution)/shard_map/ppermute | solution.py:287
  22.1 31.1 %collective-permute-start.2 = (bf16[128,1024]{1,0:T(8,128)(2,1)S(1)}, bf16[128,1024]{1,0:T(8,128)(2,1)S(1)}, u32[]{:S(2)}, u32[]{:S(2)}) collective-permute-start(bf16[128,1024]{1,0:T(8,128)(2,1)S(1)} %get-tuple-element.21), channel_id=1, source_target_pairs={{0,8},{1,12},{2,0},{3,4},{4,1},{5,5},{6,16},{7,20},{8,17},{9,21},{... | collective-permute-start | bytes 786440 | tf_op jit(solution)/shard_map/ppermute | solution.py:287
  69.0 23.6 %collective-permute-start.5 = (bf16[512,512]{1,0:T(8,128)(2,1)S(1)}, bf16[512,512]{1,0:T(8,128)(2,1)S(1)}, u32[]{:S(2)}, u32[]{:S(2)}) collective-permute-start(bf16[512,512]{1,0:T(8,128)(2,1)S(1)} %bitcast.14), channel_id=1, source_target_pairs={{0,16},{8,0},{16,8},{1,17},{9,1},{17,9},{2,18},{10,2},{18,10},{3,1... | collective-permute-start | bytes 1572872 | tf_op jit(solution)/shard_map/ppermute | solution.py:297
  71.0 25.9 %collective-permute-start.4 = (bf16[512,512]{1,0:T(8,128)(2,1)S(1)}, bf16[512,512]{1,0:T(8,128)(2,1)S(1)}, u32[]{:S(2)}, u32[]{:S(2)}) collective-permute-start(bf16[512,512]{1,0:T(8,128)(2,1)S(1)} %bitcast.15), channel_id=1, source_target_pairs={{0,8},{8,16},{16,0},{1,9},{9,17},{17,1},{2,10},{10,18},{18,2},{3,1... | collective-permute-start | bytes 1572872 | tf_op jit(solution)/shard_map/ppermute | solution.py:297
  86.8 21.4 %collective-permute-start.7 = (bf16[512,512]{1,0:T(8,128)(2,1)S(1)}, bf16[512,512]{1,0:T(8,128)(2,1)S(1)}, u32[]{:S(2)}, u32[]{:S(2)}) collective-permute-start(bf16[512,512]{1,0:T(8,128)(2,1)S(1)} %bitcast.11), channel_id=1, source_target_pairs={{0,16},{8,0},{16,8},{1,17},{9,1},{17,9},{2,18},{10,2},{18,10},{3,1... | collective-permute-start | bytes 1572872 | tf_op jit(solution)/shard_map/ppermute | solution.py:297
  89.9 27.2 %collective-permute-start.6 = (bf16[512,512]{1,0:T(8,128)(2,1)S(1)}, bf16[512,512]{1,0:T(8,128)(2,1)S(1)}, u32[]{:S(2)}, u32[]{:S(2)}) collective-permute-start(bf16[512,512]{1,0:T(8,128)(2,1)S(1)} %bitcast.12), channel_id=1, source_target_pairs={{0,8},{8,16},{16,0},{1,9},{9,17},{17,1},{2,10},{10,18},{18,2},{3,1... | collective-permute-start | bytes 1572872 | tf_op jit(solution)/shard_map/ppermute | solution.py:297
  97.0 57.9 %collective-permute-start.8 = (bf16[1536,512]{1,0:T(8,128)(2,1)S(1)}, bf16[1536,512]{1,0:T(8,128)(2,1)}, u32[]{:S(2)}, u32[]{:S(2)}) collective-permute-start(bf16[1536,512]{1,0:T(8,128)(2,1)S(1)} %pad_maximum_fusion.refs_0_.c), channel_id=1, source_target_pairs={{0,4},{4,0},{1,5},{5,1},{2,6},{6,2},{3,7},{7,3},{8,12},{12,8},{9,1... | collective-permute-start | bytes 4718600 | tf_op jit(solution)/shard_map/ppermute | solution.py:311
  117.2 49.9 %collective-permute-start.9 = (bf16[1536,512]{1,0:T(8,128)(2,1)S(1)}, bf16[1536,512]{1,0:T(8,128)(2,1)}, u32[]{:S(2)}, u32[]{:S(2)}) collective-permute-start(bf16[1536,512]{1,0:T(8,128)(2,1)S(1)} %pad_maximum_fusion.1.refs_1_.c), channel_id=1, source_target_pairs={{0,4},{4,0},{1,5},{5,1},{2,6},{6,2},{3,7},{7,3},{8,12},{12,8},{9,1... | collective-permute-start | bytes 4718600 | tf_op jit(solution)/shard_map/ppermute | solution.py:311
  119.2 20.0 %collective-permute-start.17 = (bf16[768,384]{1,0:T(8,128)(2,1)}, bf16[768,384]{1,0:T(8,128)(2,1)}, u32[]{:S(2)}, u32[]{:S(2)}) collective-permute-start(bf16[768,384]{1,0:T(8,128)(2,1)} %refs_0_.1), channel_id=1, source_target_pairs={{0,48},{24,72},{48,0},{72,24},{1,49},{25,73},{49,1},{73,25},{2,50}... | collective-permute-start | bytes 1769480 | tf_op jit(solution)/shard_map/ppermute | solution.py:289
  123.2 27.5 %collective-permute-start.16 = (bf16[768,384]{1,0:T(8,128)(2,1)}, bf16[768,384]{1,0:T(8,128)(2,1)}, u32[]{:S(2)}, u32[]{:S(2)}) collective-permute-start(bf16[768,384]{1,0:T(8,128)(2,1)} %refs_0_.1), channel_id=1, source_target_pairs={{0,24},{24,48},{48,72},{72,0},{1,25},{25,49},{49,73},{73,1},{2,26}... | collective-permute-start | bytes 1769480 | tf_op jit(solution)/shard_map/ppermute | solution.py:289
  125.9 25.4 %collective-permute-start.18 = (bf16[768,384]{1,0:T(8,128)(2,1)}, bf16[768,384]{1,0:T(8,128)(2,1)}, u32[]{:S(2)}, u32[]{:S(2)}) collective-permute-start(bf16[768,384]{1,0:T(8,128)(2,1)} %refs_0_.1), channel_id=1, source_target_pairs={{0,72},{24,0},{48,24},{72,48},{1,73},{25,1},{49,25},{73,49},{2,74}... | collective-permute-start | bytes 1769480 | tf_op jit(solution)/shard_map/ppermute | solution.py:289
  159.6 21.0 %all-to-all-start.3 = ((bf16[8,4,48,128]{3,2,1,0:T(8,128)(2,1)}), bf16[8,4,48,128]{3,2,1,0:T(8,128)(2,1)S(1)}, u32[]{:S(2)}, u32[]{:S(2)}) async-start(bf16[8,4,48,128]{3,2,1,0:T(8,128)(2,1)} %weight_part.2), calls=%async_computation.3 | async-start | bytes 786432 | tf_op jit(solution)/shard_map/all_to_all | solution.py:315
  180.6 18.4 %all-to-all-start.4 = ((bf16[8,4,48,128]{3,2,1,0:T(8,128)(2,1)}), bf16[8,4,48,128]{3,2,1,0:T(8,128)(2,1)S(1)}, u32[]{:S(2)}, u32[]{:S(2)}) async-start(bf16[8,4,48,128]{3,2,1,0:T(8,128)(2,1)} %weight_part.3), calls=%async_computation.4 | async-start | bytes 786432 | tf_op jit(solution)/shard_map/all_to_all | solution.py:315
  201.6 29.4 %all-to-all-start.5 = ((bf16[4,2,48,128]{3,2,1,0:T(8,128)(2,1)}), bf16[4,2,48,128]{3,2,1,0:T(8,128)(2,1)S(1)}, u32[]{:S(2)}, u32[]{:S(2)}) async-start(bf16[4,2,48,128]{3,2,1,0:T(8,128)(2,1)} %sum_rows.1), calls=%async_computation.5 | async-start | bytes 196608 | tf_op jit(solution)/shard_map/all_to_all | solution.py:317
  207.4 19.7 %collective-permute-start.12 = (bf16[48,256]{1,0:T(8,128)(2,1)S(1)}, bf16[48,256]{1,0:T(8,128)(2,1)S(1)}, u32[]{:S(2)}, u32[]{:S(2)}) collective-permute-start(bf16[48,256]{1,0:T(8,128)(2,1)S(1)} %pad_maximum_fusion.2.refs_0_), channel_id=1, source_target_pairs={{0,3},{1,0},{2,1},{3,2},{4,7},{5,4},{6,5},{7,6},{8,11},{9,8},{10,9... | collective-permute-start | bytes 73736 | tf_op jit(solution)/shard_map/ppermute | solution.py:303
  214.4 12.8 %collective-permute-start.11 = (bf16[48,256]{1,0:T(8,128)(2,1)S(1)}, bf16[48,256]{1,0:T(8,128)(2,1)S(1)}, u32[]{:S(2)}, u32[]{:S(2)}) collective-permute-start(bf16[48,256]{1,0:T(8,128)(2,1)S(1)} %pad_maximum_fusion.2.refs_0_), channel_id=1, source_target_pairs={{0,2},{1,3},{2,0},{3,1},{4,6},{5,7},{6,4},{7,5},{8,10},{9,11},{10,... | collective-permute-start | bytes 73736 | tf_op jit(solution)/shard_map/ppermute | solution.py:303
  231.1 25.6 %all-to-all-start.2 = ((bf16[8,4,48,256]{3,2,1,0:T(8,128)(2,1)}), bf16[8,4,48,256]{3,2,1,0:T(8,128)(2,1)S(1)}, u32[]{:S(2)}, u32[]{:S(2)}) async-start(bf16[8,4,48,256]{3,2,1,0:T(8,128)(2,1)} %spread_cols.1), calls=%async_computation.2 | async-start | bytes 1572864 | tf_op jit(solution)/shard_map/all_to_all | solution.py:305
  256.7 25.6 %all-to-all-start.6 = ((bf16[8,2,48,128]{3,2,1,0:T(8,128)(2,1)}), bf16[8,2,48,128]{3,2,1,0:T(8,128)(2,1)S(1)}, u32[]{:S(2)}, u32[]{:S(2)}) async-start(bf16[8,2,48,128]{3,2,1,0:T(8,128)(2,1)} %spread_sum.1), calls=%async_computation.6 | async-start | bytes 393216 | tf_op jit(solution)/shard_map/all_to_all | solution.py:319
  273.0 28.8 %collective-permute-start.13 = (bf16[768,384]{1,0:T(8,128)(2,1)}, bf16[768,384]{1,0:T(8,128)(2,1)S(1)}, u32[]{:S(2)}, u32[]{:S(2)}) collective-permute-start(bf16[768,384]{1,0:T(8,128)(2,1)} %get-tuple-element.13), channel_id=1, source_target_pairs={{0,24},{24,48},{48,72},{72,0},{1,25},{25,49},{49,73},{73,1},{2,26}... | collective-permute-start | bytes 1769480 | tf_op jit(solution)/shard_map/ppermute | solution.py:325
  277.1 24.8 %collective-permute-start.14 = (bf16[768,384]{1,0:T(8,128)(2,1)}, bf16[768,384]{1,0:T(8,128)(2,1)S(1)}, u32[]{:S(2)}, u32[]{:S(2)}) collective-permute-start(bf16[768,384]{1,0:T(8,128)(2,1)} %get-tuple-element.14), channel_id=1, source_target_pairs={{0,48},{24,72},{48,0},{72,24},{1,49},{25,73},{49,1},{73,25},{2,50}... | collective-permute-start | bytes 1769480 | tf_op jit(solution)/shard_map/ppermute | solution.py:325
  279.0 27.8 %collective-permute-start.15 = (bf16[768,384]{1,0:T(8,128)(2,1)}, bf16[768,384]{1,0:T(8,128)(2,1)S(1)}, u32[]{:S(2)}, u32[]{:S(2)}) collective-permute-start(bf16[768,384]{1,0:T(8,128)(2,1)} %get-tuple-element.15), channel_id=1, source_target_pairs={{0,72},{24,0},{48,24},{72,48},{1,73},{25,1},{49,25},{73,49},{2,74}... | collective-permute-start | bytes 1769480 | tf_op jit(solution)/shard_map/ppermute | solution.py:325
  284.9 30.4 %all-to-all-start.7 = ((bf16[4,2,384,128]{3,2,1,0:T(8,128)(2,1)}), bf16[4,2,384,128]{3,2,1,0:T(8,128)(2,1)S(1)}, u32[]{:S(2)}, u32[]{:S(2)}) async-start(bf16[4,2,384,128]{3,2,1,0:T(8,128)(2,1)} %spread_rows.1), calls=%async_computation.7 | async-start | bytes 1572864 | tf_op jit(solution)/shard_map/all_to_all | solution.py:321
  (20 other events, 186.9 us)
where the time goes:
time: 320 us; the launch traced here: 318 us
  waiting for transfers between devices  133 us (42%)
  starting transfers between devices  112 us (35%)
  Pallas kernels  40.2 us (13%)
  blocking collectives  24.6 us (8%)
  local copies, waits for them, and re-layouts  7.17 us (2%)
    ppermute x4, waiting for transfers between devices, per_device(): lax.ppermute(sends[k], ('zl', 'core', 'zh'), spread_pairs(k))  26.6 us
    all_to_all x2, blocking collectives, per_device(): part = lax.all_to_all(mine[h], 'x', 0, 0)  24.6 us
    ppermute x4, starting transfers between devices, per_device(): lax.ppermute(sends[k], ('zl', 'core', 'zh'), spread_pairs(k))  24.6 us
    ppermute x4, waiting for transfers between devices, per_device(): lax.ppermute(part, 'zl', ring(ZL, k))  22.4 us
    all_to_all x2, waiting for transfers between devices, per_device(): parts.append(lax.all_to_all(part, 'y', 0, 0))  22.3 us
    ppermute x3, waiting for transfers between devices, per_device(): lax.ppermute(heads, 'x', ring(X, k))  21.6 us
    ppermute x3, starting transfers between devices, per_device(): w_far = [lax.ppermute(w_part, 'zh', ring(ZH, k)) for k in range(1, ZH)]  19.7 us
    all_to_all x1, waiting for transfers between devices, per_device(): w_y = lax.all_to_all(w_y, 'y', 0, 0)  19.1 us
  transfers between devices with their start and end apart: 25, of which 16 were waited for; matrix products, arithmetic and copies ran while one was open for 0% of the time, Pallas kernels for 11%

commit v1 on v0

--- a/solution.py
+++ b/solution.py
@@ -123,25 +123,33 @@
     )(pieces)
 
 
-def weight_part(heads_t, own, oth):
+def weight_part(heads_t, own, oth, before=None):
     hid = heads_t[0].shape[0]
     rows = hid // Y
-
-    def kernel(a, b, c, d, out):
+    both = before is not None
+
+    def kernel(a, b, c, d, *refs):
+        out = refs[-1]
         acc = jnp.dot(a[...], c[...], preferred_element_type=jnp.float32)
         acc += jnp.dot(b[...], d[...], preferred_element_type=jnp.float32)
         acc = acc.astype(out.dtype)
         for y in range(Y):
             for col in range(ZH):
-                out[y, col] = acc[y * rows:(y + 1) * rows, col * LANE:(col + 1) * LANE]
-
-    return pl.pallas_call(
-        kernel,
-        out_shape=jax.ShapeDtypeStruct((Y, ZH, rows, LANE), own.dtype),
-        in_specs=[VMEM] * 4,
+                v = acc[y * rows:(y + 1) * rows, col * LANE:(col + 1) * LANE]
+                if both:
+                    out[y, col, 0] = refs[0][y, col]
+                    out[y, col, 1] = v
+                else:
+                    out[y, col] = v
+
+    shape = (Y, ZH, CHUNKS, rows, LANE) if both else (Y, ZH, rows, LANE)
+    return pl.pallas_call(
+        kernel,
+        out_shape=jax.ShapeDtypeStruct(shape, own.dtype),
+        in_specs=[VMEM] * (5 if both else 4),
         out_specs=VMEM,
         name="weight_part",
-    )(*heads_t, own, oth)
+    )(*heads_t, own, oth, *((before,) if both else ()))
 
 
 def heads_part(owns, oths, weight, rows, at):
@@ -198,21 +206,17 @@
 
 
 def sum_rows(parts):
-    _, _, rows, _ = parts[0].shape
-
-    def kernel(*refs):
-        out = refs[-1]
-        for h in range(CHUNKS):
-            for col in range(ZH):
-                out[col, h] = jnp.sum(refs[h][:, col].astype(jnp.float32), axis=0).astype(out.dtype)
-
-    return pl.pallas_call(
-        kernel,
-        out_shape=jax.ShapeDtypeStruct((ZH, CHUNKS, rows, LANE), parts[0].dtype),
-        in_specs=[VMEM] * CHUNKS,
+    def kernel(src, out):
+        for col in range(ZH):
+            out[col] = jnp.sum(src[:, col].astype(jnp.float32), axis=0).astype(out.dtype)
+
+    return pl.pallas_call(
+        kernel,
+        out_shape=jax.ShapeDtypeStruct(parts.shape[1:], parts.dtype),
+        in_specs=[VMEM],
         out_specs=VMEM,
         name="sum_rows",
-    )(*parts)
+    )(parts)
 
 
 def spread_sum(parts):
@@ -305,15 +309,16 @@
     w_y = lax.all_to_all(w_y, "y", 0, 0)
     w_y = weight_rows(w_y)
 
-    owns, oths, parts = [], [], []
+    owns, oths = [], []
     for h in range(CHUNKS):
         own = jnp.concatenate(near[h], axis=0)
         oth = lax.ppermute(own, "core", ring(CORE, 1))
         owns.append(own)
         oths.append(oth)
-        part = weight_part(heads_t, own, oth)
-        parts.append(lax.all_to_all(part, "y", 0, 0))
-    r = sum_rows(parts)
+    first = weight_part(heads_t, owns[0], oths[0])
+    r = weight_part(heads_t, owns[1], oths[1], first)
+    r = lax.all_to_all(r, "y", 0, 0)
+    r = sum_rows(r)
     r = lax.all_to_all(r, "zh", 0, 0)
     r = spread_sum(r)
     r = lax.all_to_all(r, "y", 0, 0)

time: 320 us -> 321 us (level)
  the two profiles are of different devices: /device:TPU:78 before, /device:TPU:10 now
where the time goes in v1:
time: 321 us; the launch traced here: 319 us
  waiting for transfers between devices  137 us (43%)
  starting transfers between devices  119 us (37%)
  Pallas kernels  40.4 us (13%)
  blocking collectives  11.4 us (4%)
  local copies, waits for them, and re-layouts  7.35 us (2%)
    ppermute x4, waiting for transfers between devices, per_device(): lax.ppermute(part, 'zl', ring(ZL, k))  33.2 us
    ppermute x4, starting transfers between devices, per_device(): lax.ppermute(sends[k], ('zl', 'core', 'zh'), spread_pairs(k))  24.4 us
    all_to_all x2, waiting for transfers between devices, per_device(): r = lax.all_to_all(r, 'y', 0, 0)  21.8 us
    ppermute x3, waiting for transfers between devices, per_device(): lax.ppermute(heads, 'x', ring(X, k))  21.6 us
    ppermute x4, waiting for transfers between devices, per_device(): lax.ppermute(sends[k], ('zl', 'core', 'zh'), spread_pairs(k))  21.2 us
    ppermute x4, starting transfers between devices, per_device(): lax.ppermute(part, 'zl', ring(ZL, k))  21.1 us
    ppermute x3, starting transfers between devices, per_device(): w_far = [lax.ppermute(w_part, 'zh', ring(ZH, k)) for k in range(1, ZH)]  18.5 us
    all_to_all x1, waiting for transfers between devices, per_device(): w_y = lax.all_to_all(w_y, 'y', 0, 0)  18.4 us
  transfers between devices with their start and end apart: 25, of which 14 were waited for; matrix products, arithmetic and copies ran while one was open for 1% of the time, Pallas kernels for 9%

profile of v1, /device:TPU:10, one launch (start us, length us, event | category | flops | bytes accessed | tf_op | source)
XLA Modules:
  0.0 319.1 jit_solution(4185938732923275563)
XLA Ops:
  5.7 5.6 %collective-permute-start.1 = (bf16[128,1024]{1,0:T(8,128)(2,1)S(1)}, bf16[128,1024]{1,0:T(8,128)(2,1)S(1)}, u32[]{:S(2)}, u32[]{:S(2)}) collective-permute-start(bf16[128,1024]{1,0:T(8,128)(2,1)S(1)} %get-tuple-element.19), channel_id=1, source_target_pairs={{0,4},{1,8},{2,12},{3,0},{4,20},{5,1},{6,5},{7,16},{8,13},{9,17},{... | collective-permute-start | bytes 786440 | tf_op jit(solution)/shard_map/ppermute | solution.py:291
  12.0 14.3 %collective-permute-start.2 = (bf16[128,1024]{1,0:T(8,128)(2,1)S(1)}, bf16[128,1024]{1,0:T(8,128)(2,1)S(1)}, u32[]{:S(2)}, u32[]{:S(2)}) collective-permute-start(bf16[128,1024]{1,0:T(8,128)(2,1)S(1)} %get-tuple-element.21), channel_id=1, source_target_pairs={{0,8},{1,12},{2,0},{3,4},{4,1},{5,5},{6,16},{7,20},{8,17},{9,21},{... | collective-permute-start | bytes 786440 | tf_op jit(solution)/shard_map/ppermute | solution.py:291
  26.4 21.2 %collective-permute-done.1.refs_1_ = bf16[128,1024]{1,0:T(8,128)(2,1)S(1)} collective-permute-done((bf16[128,1024]{1,0:T(8,128)(2,1)S(1)}, bf16[128,1024]{1,0:T(8,128)(2,1)S(1)}, u32[]{:S(2)}, u32[]{:S(2)}) %collective-permute-start.1) | collective-permute-done | bytes 262176 | tf_op jit(solution)/shard_map/ppermute | solution.py:291
  50.9 11.4 %all_to_all.35 = bf16[4,128,512]{2,1,0:T(8,128)(2,1)S(1)} all-to-all(bf16[4,128,512]{2,1,0:T(8,128)(2,1)} %get-tuple-element.10), channel_id=1, replica_groups=mesh['y'=8,'x'=4,'zl'=3,'core'=2,'zh'=4] {'x'}, dimensions={0} | all-to-all | bytes 1048576 | tf_op jit(solution)/shard_map/all_to_all | solution.py:299
  62.4 4.9 %all-to-all-start.1 = ((bf16[4,128,512]{2,1,0:T(8,128)(2,1)}), bf16[4,128,512]{2,1,0:T(8,128)(2,1)S(1)}, u32[]{:S(2)}, u32[]{:S(2)}) async-start(bf16[4,128,512]{2,1,0:T(8,128)(2,1)} %get-tuple-element.11), calls=%async_computation.1 | async-start | bytes 1048576 | tf_op jit(solution)/shard_map/all_to_all | solution.py:299
  67.3 11.5 %collective-permute-start.5 = (bf16[512,512]{1,0:T(8,128)(2,1)S(1)}, bf16[512,512]{1,0:T(8,128)(2,1)S(1)}, u32[]{:S(2)}, u32[]{:S(2)}) collective-permute-start(bf16[512,512]{1,0:T(8,128)(2,1)S(1)} %bitcast.14), channel_id=1, source_target_pairs={{0,16},{8,0},{16,8},{1,17},{9,1},{17,9},{2,18},{10,2},{18,10},{3,1... | collective-permute-start | bytes 1572872 | tf_op jit(solution)/shard_map/ppermute | solution.py:301
  88.4 13.0 %collective-permute-done.5 = bf16[512,512]{1,0:T(8,128)(2,1)S(1)} collective-permute-done((bf16[512,512]{1,0:T(8,128)(2,1)S(1)}, bf16[512,512]{1,0:T(8,128)(2,1)S(1)}, u32[]{:S(2)}, u32[]{:S(2)}) %collective-permute-start.5) | collective-permute-done | bytes 524320 | tf_op jit(solution)/shard_map/ppermute | solution.py:301
  107.6 7.4 %collective-permute-done.7 = bf16[512,512]{1,0:T(8,128)(2,1)S(1)} collective-permute-done((bf16[512,512]{1,0:T(8,128)(2,1)S(1)}, bf16[512,512]{1,0:T(8,128)(2,1)S(1)}, u32[]{:S(2)}, u32[]{:S(2)}) %collective-permute-start.7) | collective-permute-done | bytes 524320 | tf_op jit(solution)/shard_map/ppermute | solution.py:301
  114.9 9.8 %collective-permute-done.6 = bf16[512,512]{1,0:T(8,128)(2,1)S(1)} collective-permute-done((bf16[512,512]{1,0:T(8,128)(2,1)S(1)}, bf16[512,512]{1,0:T(8,128)(2,1)S(1)}, u32[]{:S(2)}, u32[]{:S(2)}) %collective-permute-start.6) | collective-permute-done | bytes 524320 | tf_op jit(solution)/shard_map/ppermute | solution.py:301
  138.3 9.4 %collective-permute-done.17.refs_2_ = bf16[768,384]{1,0:T(8,128)(2,1)} collective-permute-done((bf16[768,384]{1,0:T(8,128)(2,1)}, bf16[768,384]{1,0:T(8,128)(2,1)}, u32[]{:S(2)}, u32[]{:S(2)}) %collective-permute-start.17) | collective-permute-done | bytes 589856 | tf_op jit(solution)/shard_map/ppermute | solution.py:293
  147.8 12.2 %collective-permute-done.16.refs_1_ = bf16[768,384]{1,0:T(8,128)(2,1)} collective-permute-done((bf16[768,384]{1,0:T(8,128)(2,1)}, bf16[768,384]{1,0:T(8,128)(2,1)}, u32[]{:S(2)}, u32[]{:S(2)}) %collective-permute-start.16) | collective-permute-done | bytes 589856 | tf_op jit(solution)/shard_map/ppermute | solution.py:293
  168.3 5.0 %weight_part.3 = bf16[8,4,2,48,128]{4,3,2,1,0:T(8,128)(2,1)} custom-call(bf16[384,1536]{1,0:T(8,128)(2,1)} %get-tuple-element.16.a, bf16[384,1536]{1,0:T(8,128)(2,1)} %get-tuple-element.17.b, bf16[1536,512]{1,0:T(8,128)(2,1)} %copy-done.1, bf16[1536,512]{1,0:T(8,128)(2,1)} %collective-permute-done.9.refs_3_.d, bf16[8,4,48,128]{3,2,1,0:T(8,128)(2,1)} %weight_part.2.refs_0_), custom_call_target="tpu_custom_call" | custom-call | tf_op jit(solution)/shard_map/weight_part/pallas_call | solution.py:146
  173.3 7.5 %all-to-all-start.3 = ((bf16[8,4,2,48,128]{4,3,2,1,0:T(8,128)(2,1)}), bf16[8,4,2,48,128]{4,3,2,1,0:T(8,128)(2,1)S(1)}, u32[]{:S(2)}, u32[]{:S(2)}) async-start(bf16[8,4,2,48,128]{4,3,2,1,0:T(8,128)(2,1)} %weight_part.3), calls=%async_computation.3 | async-start | bytes 1572864 | tf_op jit(solution)/shard_map/all_to_all | solution.py:320
  180.8 21.8 %all-to-all-done.3.src = bf16[8,4,2,48,128]{4,3,2,1,0:T(8,128)(2,1)S(1)} async-done(((bf16[8,4,2,48,128]{4,3,2,1,0:T(8,128)(2,1)}), bf16[8,4,2,48,128]{4,3,2,1,0:T(8,128)(2,1)S(1)}, u32[]{:S(2)}, u32[]{:S(2)}) %all-to-all-start.3) | async-done | bytes 786464 | tf_op jit(solution)/shard_map/all_to_all | solution.py:320
  210.3 6.9 %collective-permute-start.12 = (bf16[48,256]{1,0:T(8,128)(2,1)S(1)}, bf16[48,256]{1,0:T(8,128)(2,1)S(1)}, u32[]{:S(2)}, u32[]{:S(2)}) collective-permute-start(bf16[48,256]{1,0:T(8,128)(2,1)S(1)} %pad_maximum_fusion.2.refs_0_), channel_id=1, source_target_pairs={{0,3},{1,0},{2,1},{3,2},{4,7},{5,4},{6,5},{7,6},{8,11},{9,8},{10,9... | collective-permute-start | bytes 73736 | tf_op jit(solution)/shard_map/ppermute | solution.py:307
  217.3 5.8 %collective-permute-start.11 = (bf16[48,256]{1,0:T(8,128)(2,1)S(1)}, bf16[48,256]{1,0:T(8,128)(2,1)S(1)}, u32[]{:S(2)}, u32[]{:S(2)}) collective-permute-start(bf16[48,256]{1,0:T(8,128)(2,1)S(1)} %pad_maximum_fusion.2.refs_0_), channel_id=1, source_target_pairs={{0,2},{1,3},{2,0},{3,1},{4,6},{5,7},{6,4},{7,5},{8,10},{9,11},{10,... | collective-permute-start | bytes 73736 | tf_op jit(solution)/shard_map/ppermute | solution.py:307
  223.1 5.8 %collective-permute-start.10 = (bf16[48,256]{1,0:T(8,128)(2,1)S(1)}, bf16[48,256]{1,0:T(8,128)(2,1)S(1)}, u32[]{:S(2)}, u32[]{:S(2)}) collective-permute-start(bf16[48,256]{1,0:T(8,128)(2,1)S(1)} %pad_maximum_fusion.2.refs_0_), channel_id=1, source_target_pairs={{0,1},{1,2},{2,3},{3,0},{4,5},{5,6},{6,7},{7,4},{8,9},{9,10},{10,1... | collective-permute-start | bytes 73736 | tf_op jit(solution)/shard_map/ppermute | solution.py:307
  234.4 4.8 %all-to-all-start.2 = ((bf16[8,4,48,256]{3,2,1,0:T(8,128)(2,1)}), bf16[8,4,48,256]{3,2,1,0:T(8,128)(2,1)S(1)}, u32[]{:S(2)}, u32[]{:S(2)}) async-start(bf16[8,4,48,256]{3,2,1,0:T(8,128)(2,1)} %spread_cols.1), calls=%async_computation.2 | async-start | bytes 1572864 | tf_op jit(solution)/shard_map/all_to_all | solution.py:309
  240.9 18.4 %all-to-all-done.2.src = bf16[8,4,48,256]{3,2,1,0:T(8,128)(2,1)S(1)} async-done(((bf16[8,4,48,256]{3,2,1,0:T(8,128)(2,1)}), bf16[8,4,48,256]{3,2,1,0:T(8,128)(2,1)S(1)}, u32[]{:S(2)}, u32[]{:S(2)}) %all-to-all-start.2) | async-done | bytes 786464 | tf_op jit(solution)/shard_map/all_to_all | solution.py:309
  259.2 4.8 %all-to-all-start.5 = ((bf16[8,2,48,128]{3,2,1,0:T(8,128)(2,1)}), bf16[8,2,48,128]{3,2,1,0:T(8,128)(2,1)S(1)}, u32[]{:S(2)}, u32[]{:S(2)}) async-start(bf16[8,2,48,128]{3,2,1,0:T(8,128)(2,1)} %spread_sum.1), calls=%async_computation.5 | async-start | bytes 393216 | tf_op jit(solution)/shard_map/all_to_all | solution.py:324
  266.2 9.4 %heads_part.1 = (bf16[768,384]{1,0:T(8,128)(2,1)}, bf16[768,384]{1,0:T(8,128)(2,1)}, bf16[768,384]{1,0:T(8,128)(2,1)}, bf16[768,384]{1,0:T(8,128)(2,1)}) custom-call(s32[1]{0:T(128)} %bitcast.at_ref, s32[6]{0:T(128)} %stack.34.rows_ref, bf16[1536,512]{1,0:T(8,128)(2,1)} %copy-done, bf16[1536,512]{1,0:T(8,128)(2,1)} %copy-done.1, ...), custom_call_target="tpu_custom_call" | custom-call | tf_op jit(solution)/shard_map/heads_part/pallas_call | solution.py:179
  288.6 5.0 %all-to-all-start.6 = ((bf16[4,2,384,128]{3,2,1,0:T(8,128)(2,1)}), bf16[4,2,384,128]{3,2,1,0:T(8,128)(2,1)S(1)}, u32[]{:S(2)}, u32[]{:S(2)}) async-start(bf16[4,2,384,128]{3,2,1,0:T(8,128)(2,1)} %spread_rows.1), calls=%async_computation.6 | async-start | bytes 1572864 | tf_op jit(solution)/shard_map/all_to_all | solution.py:326
  293.6 6.8 %collective-permute-done.13.refs_1_ = bf16[768,384]{1,0:T(8,128)(2,1)S(1)} collective-permute-done((bf16[768,384]{1,0:T(8,128)(2,1)}, bf16[768,384]{1,0:T(8,128)(2,1)S(1)}, u32[]{:S(2)}, u32[]{:S(2)}) %collective-permute-start.13) | collective-permute-done | bytes 589856 | tf_op jit(solution)/shard_map/ppermute | solution.py:330
  300.4 8.1 %collective-permute-done.15.refs_3_ = bf16[768,384]{1,0:T(8,128)(2,1)S(1)} collective-permute-done((bf16[768,384]{1,0:T(8,128)(2,1)}, bf16[768,384]{1,0:T(8,128)(2,1)S(1)}, u32[]{:S(2)}, u32[]{:S(2)}) %collective-permute-start.15) | collective-permute-done | bytes 589856 | tf_op jit(solution)/shard_map/ppermute | solution.py:330
  (83 shorter events, 87.2 us)
Async XLA Ops:
  2.0 24.4 %collective-permute-start.3 = (bf16[128,1024]{1,0:T(8,128)(2,1)S(1)}, bf16[128,1024]{1,0:T(8,128)(2,1)S(1)}, u32[]{:S(2)}, u32[]{:S(2)}) collective-permute-start(bf16[128,1024]{1,0:T(8,128)(2,1)S(1)} %get-tuple-element.18), channel_id=1, source_target_pairs={{0,12},{1,0},{2,4},{3,8},{4,5},{5,16},{6,20},{7,1},{8,21},{9,9},{1... | collective-permute-start | bytes 786440 | tf_op jit(solution)/shard_map/ppermute | solution.py:291
  5.7 41.9 %collective-permute-start.1 = (bf16[128,1024]{1,0:T(8,128)(2,1)S(1)}, bf16[128,1024]{1,0:T(8,128)(2,1)S(1)}, u32[]{:S(2)}, u32[]{:S(2)}) collective-permute-start(bf16[128,1024]{1,0:T(8,128)(2,1)S(1)} %get-tuple-element.19), channel_id=1, source_target_pairs={{0,4},{1,8},{2,12},{3,0},{4,20},{5,1},{6,5},{7,16},{8,13},{9,17},{... | collective-permute-start | bytes 786440 | tf_op jit(solution)/shard_map/ppermute | solution.py:291
  11.3 36.3 %collective-permute-start = (bf16[128,1024]{1,0:T(8,128)(2,1)S(1)}, bf16[128,1024]{1,0:T(8,128)(2,1)S(1)}, u32[]{:S(2)}, u32[]{:S(2)}) collective-permute-start(bf16[128,1024]{1,0:T(8,128)(2,1)S(1)} %get-tuple-element.20), channel_id=1, source_target_pairs={{0,0},{1,4},{2,8},{3,12},{4,16},{5,20},{6,1},{7,5},{8,9},{9,13},{1... | collective-permute-start | bytes 786440 | tf_op jit(solution)/shard_map/ppermute | solution.py:291
  12.0 35.6 %collective-permute-start.2 = (bf16[128,1024]{1,0:T(8,128)(2,1)S(1)}, bf16[128,1024]{1,0:T(8,128)(2,1)S(1)}, u32[]{:S(2)}, u32[]{:S(2)}) collective-permute-start(bf16[128,1024]{1,0:T(8,128)(2,1)S(1)} %get-tuple-element.21), channel_id=1, source_target_pairs={{0,8},{1,12},{2,0},{3,4},{4,1},{5,5},{6,16},{7,20},{8,17},{9,21},{... | collective-permute-start | bytes 786440 | tf_op jit(solution)/shard_map/ppermute | solution.py:291
  62.4 18.4 %all-to-all-start.1 = ((bf16[4,128,512]{2,1,0:T(8,128)(2,1)}), bf16[4,128,512]{2,1,0:T(8,128)(2,1)S(1)}, u32[]{:S(2)}, u32[]{:S(2)}) async-start(bf16[4,128,512]{2,1,0:T(8,128)(2,1)} %get-tuple-element.11), calls=%async_computation.1 | async-start | bytes 1048576 | tf_op jit(solution)/shard_map/all_to_all | solution.py:299
  67.3 34.1 %collective-permute-start.5 = (bf16[512,512]{1,0:T(8,128)(2,1)S(1)}, bf16[512,512]{1,0:T(8,128)(2,1)S(1)}, u32[]{:S(2)}, u32[]{:S(2)}) collective-permute-start(bf16[512,512]{1,0:T(8,128)(2,1)S(1)} %bitcast.14), channel_id=1, source_target_pairs={{0,16},{8,0},{16,8},{1,17},{9,1},{17,9},{2,18},{10,2},{18,10},{3,1... | collective-permute-start | bytes 1572872 | tf_op jit(solution)/shard_map/ppermute | solution.py:301
  78.7 25.7 %collective-permute-start.4 = (bf16[512,512]{1,0:T(8,128)(2,1)S(1)}, bf16[512,512]{1,0:T(8,128)(2,1)}, u32[]{:S(2)}, u32[]{:S(2)}) collective-permute-start(bf16[512,512]{1,0:T(8,128)(2,1)S(1)} %bitcast.15), channel_id=1, source_target_pairs={{0,8},{8,16},{16,0},{1,9},{9,17},{17,1},{2,10},{10,18},{18,2},{3,1... | collective-permute-start | bytes 1572872 | tf_op jit(solution)/shard_map/ppermute | solution.py:301
  80.8 34.1 %collective-permute-start.7 = (bf16[512,512]{1,0:T(8,128)(2,1)S(1)}, bf16[512,512]{1,0:T(8,128)(2,1)S(1)}, u32[]{:S(2)}, u32[]{:S(2)}) collective-permute-start(bf16[512,512]{1,0:T(8,128)(2,1)S(1)} %bitcast.11), channel_id=1, source_target_pairs={{0,16},{8,0},{16,8},{1,17},{9,1},{17,9},{2,18},{10,2},{18,10},{3,1... | collective-permute-start | bytes 1572872 | tf_op jit(solution)/shard_map/ppermute | solution.py:301
  85.5 39.2 %collective-permute-start.6 = (bf16[512,512]{1,0:T(8,128)(2,1)S(1)}, bf16[512,512]{1,0:T(8,128)(2,1)S(1)}, u32[]{:S(2)}, u32[]{:S(2)}) collective-permute-start(bf16[512,512]{1,0:T(8,128)(2,1)S(1)} %bitcast.12), channel_id=1, source_target_pairs={{0,8},{8,16},{16,0},{1,9},{9,17},{17,1},{2,10},{10,18},{18,2},{3,1... | collective-permute-start | bytes 1572872 | tf_op jit(solution)/shard_map/ppermute | solution.py:301
  105.6 57.9 %collective-permute-start.8 = (bf16[1536,512]{1,0:T(8,128)(2,1)S(1)}, bf16[1536,512]{1,0:T(8,128)(2,1)}, u32[]{:S(2)}, u32[]{:S(2)}) collective-permute-start(bf16[1536,512]{1,0:T(8,128)(2,1)S(1)} %pad_maximum_fusion.refs_0_.c), channel_id=1, source_target_pairs={{0,4},{4,0},{1,5},{5,1},{2,6},{6,2},{3,7},{7,3},{8,12},{12,8},{9,1... | collective-permute-start | bytes 4718600 | tf_op jit(solution)/shard_map/ppermute | solution.py:315
  125.9 42.4 %collective-permute-start.9 = (bf16[1536,512]{1,0:T(8,128)(2,1)S(1)}, bf16[1536,512]{1,0:T(8,128)(2,1)}, u32[]{:S(2)}, u32[]{:S(2)}) collective-permute-start(bf16[1536,512]{1,0:T(8,128)(2,1)S(1)} %pad_maximum_fusion.1.refs_1_.c), channel_id=1, source_target_pairs={{0,4},{4,0},{1,5},{5,1},{2,6},{6,2},{3,7},{7,3},{8,12},{12,8},{9,1... | collective-permute-start | bytes 4718600 | tf_op jit(solution)/shard_map/ppermute | solution.py:315
  127.8 20.0 %collective-permute-start.17 = (bf16[768,384]{1,0:T(8,128)(2,1)}, bf16[768,384]{1,0:T(8,128)(2,1)}, u32[]{:S(2)}, u32[]{:S(2)}) collective-permute-start(bf16[768,384]{1,0:T(8,128)(2,1)} %refs_0_.1), channel_id=1, source_target_pairs={{0,48},{24,72},{48,0},{72,24},{1,49},{25,73},{49,1},{73,25},{2,50}... | collective-permute-start | bytes 1769480 | tf_op jit(solution)/shard_map/ppermute | solution.py:293
  131.8 28.1 %collective-permute-start.16 = (bf16[768,384]{1,0:T(8,128)(2,1)}, bf16[768,384]{1,0:T(8,128)(2,1)}, u32[]{:S(2)}, u32[]{:S(2)}) collective-permute-start(bf16[768,384]{1,0:T(8,128)(2,1)} %refs_0_.1), channel_id=1, source_target_pairs={{0,24},{24,48},{48,72},{72,0},{1,25},{25,49},{49,73},{73,1},{2,26}... | collective-permute-start | bytes 1769480 | tf_op jit(solution)/shard_map/ppermute | solution.py:293
  133.7 26.2 %collective-permute-start.18 = (bf16[768,384]{1,0:T(8,128)(2,1)}, bf16[768,384]{1,0:T(8,128)(2,1)}, u32[]{:S(2)}, u32[]{:S(2)}) collective-permute-start(bf16[768,384]{1,0:T(8,128)(2,1)} %refs_0_.1), channel_id=1, source_target_pairs={{0,72},{24,0},{48,24},{72,48},{1,73},{25,1},{49,25},{73,49},{2,74}... | collective-permute-start | bytes 1769480 | tf_op jit(solution)/shard_map/ppermute | solution.py:293
  173.3 29.4 %all-to-all-start.3 = ((bf16[8,4,2,48,128]{4,3,2,1,0:T(8,128)(2,1)}), bf16[8,4,2,48,128]{4,3,2,1,0:T(8,128)(2,1)S(1)}, u32[]{:S(2)}, u32[]{:S(2)}) async-start(bf16[8,4,2,48,128]{4,3,2,1,0:T(8,128)(2,1)} %weight_part.3), calls=%async_computation.3 | async-start | bytes 1572864 | tf_op jit(solution)/shard_map/all_to_all | solution.py:320
  205.4 29.0 %all-to-all-start.4 = ((bf16[4,2,48,128]{3,2,1,0:T(8,128)(2,1)}), bf16[4,2,48,128]{3,2,1,0:T(8,128)(2,1)S(1)}, u32[]{:S(2)}, u32[]{:S(2)}) async-start(bf16[4,2,48,128]{3,2,1,0:T(8,128)(2,1)} %sum_rows.1), calls=%async_computation.4 | async-start | bytes 196608 | tf_op jit(solution)/shard_map/all_to_all | solution.py:322
  210.3 18.5 %collective-permute-start.12 = (bf16[48,256]{1,0:T(8,128)(2,1)S(1)}, bf16[48,256]{1,0:T(8,128)(2,1)S(1)}, u32[]{:S(2)}, u32[]{:S(2)}) collective-permute-start(bf16[48,256]{1,0:T(8,128)(2,1)S(1)} %pad_maximum_fusion.2.refs_0_), channel_id=1, source_target_pairs={{0,3},{1,0},{2,1},{3,2},{4,7},{5,4},{6,5},{7,6},{8,11},{9,8},{10,9... | collective-permute-start | bytes 73736 | tf_op jit(solution)/shard_map/ppermute | solution.py:307
  217.3 12.3 %collective-permute-start.11 = (bf16[48,256]{1,0:T(8,128)(2,1)S(1)}, bf16[48,256]{1,0:T(8,128)(2,1)S(1)}, u32[]{:S(2)}, u32[]{:S(2)}) collective-permute-start(bf16[48,256]{1,0:T(8,128)(2,1)S(1)} %pad_maximum_fusion.2.refs_0_), channel_id=1, source_target_pairs={{0,2},{1,3},{2,0},{3,1},{4,6},{5,7},{6,4},{7,5},{8,10},{9,11},{10,... | collective-permute-start | bytes 73736 | tf_op jit(solution)/shard_map/ppermute | solution.py:307
  234.4 24.8 %all-to-all-start.2 = ((bf16[8,4,48,256]{3,2,1,0:T(8,128)(2,1)}), bf16[8,4,48,256]{3,2,1,0:T(8,128)(2,1)S(1)}, u32[]{:S(2)}, u32[]{:S(2)}) async-start(bf16[8,4,48,256]{3,2,1,0:T(8,128)(2,1)} %spread_cols.1), calls=%async_computation.2 | async-start | bytes 1572864 | tf_op jit(solution)/shard_map/all_to_all | solution.py:309
  259.2 26.8 %all-to-all-start.5 = ((bf16[8,2,48,128]{3,2,1,0:T(8,128)(2,1)}), bf16[8,2,48,128]{3,2,1,0:T(8,128)(2,1)S(1)}, u32[]{:S(2)}, u32[]{:S(2)}) async-start(bf16[8,2,48,128]{3,2,1,0:T(8,128)(2,1)} %spread_sum.1), calls=%async_computation.5 | async-start | bytes 393216 | tf_op jit(solution)/shard_map/all_to_all | solution.py:324
  275.6 24.8 %collective-permute-start.13 = (bf16[768,384]{1,0:T(8,128)(2,1)}, bf16[768,384]{1,0:T(8,128)(2,1)S(1)}, u32[]{:S(2)}, u32[]{:S(2)}) collective-permute-start(bf16[768,384]{1,0:T(8,128)(2,1)} %get-tuple-element.13), channel_id=1, source_target_pairs={{0,24},{24,48},{48,72},{72,0},{1,25},{25,49},{49,73},{73,1},{2,26}... | collective-permute-start | bytes 1769480 | tf_op jit(solution)/shard_map/ppermute | solution.py:330
  279.0 21.4 %collective-permute-start.14 = (bf16[768,384]{1,0:T(8,128)(2,1)}, bf16[768,384]{1,0:T(8,128)(2,1)S(1)}, u32[]{:S(2)}, u32[]{:S(2)}) collective-permute-start(bf16[768,384]{1,0:T(8,128)(2,1)} %get-tuple-element.14), channel_id=1, source_target_pairs={{0,48},{24,72},{48,0},{72,24},{1,49},{25,73},{49,1},{73,25},{2,50}... | collective-permute-start | bytes 1769480 | tf_op jit(solution)/shard_map/ppermute | solution.py:330
  281.8 26.7 %collective-permute-start.15 = (bf16[768,384]{1,0:T(8,128)(2,1)}, bf16[768,384]{1,0:T(8,128)(2,1)S(1)}, u32[]{:S(2)}, u32[]{:S(2)}) collective-permute-start(bf16[768,384]{1,0:T(8,128)(2,1)} %get-tuple-element.15), channel_id=1, source_target_pairs={{0,72},{24,0},{48,24},{72,48},{1,73},{25,1},{49,25},{73,49},{2,74}... | collective-permute-start | bytes 1769480 | tf_op jit(solution)/shard_map/ppermute | solution.py:330
  288.6 27.4 %all-to-all-start.6 = ((bf16[4,2,384,128]{3,2,1,0:T(8,128)(2,1)}), bf16[4,2,384,128]{3,2,1,0:T(8,128)(2,1)S(1)}, u32[]{:S(2)}, u32[]{:S(2)}) async-start(bf16[4,2,384,128]{3,2,1,0:T(8,128)(2,1)} %spread_rows.1), calls=%async_computation.6 | async-start | bytes 1572864 | tf_op jit(solution)/shard_map/all_to_all | solution.py:326
  (20 other events, 177.0 us)

commit v2 on v1

--- a/solution.py
+++ b/solution.py
@@ -205,20 +205,6 @@
     )(*parts)
 
 
-def sum_rows(parts):
-    def kernel(src, out):
-        for col in range(ZH):
-            out[col] = jnp.sum(src[:, col].astype(jnp.float32), axis=0).astype(out.dtype)
-
-    return pl.pallas_call(
-        kernel,
-        out_shape=jax.ShapeDtypeStruct(parts.shape[1:], parts.dtype),
-        in_specs=[VMEM],
-        out_specs=VMEM,
-        name="sum_rows",
-    )(parts)
-
-
 def spread_sum(parts):
     shape = (Y,) + parts.shape[1:]
 
@@ -317,9 +303,7 @@
         oths.append(oth)
     first = weight_part(heads_t, owns[0], oths[0])
     r = weight_part(heads_t, owns[1], oths[1], first)
-    r = lax.all_to_all(r, "y", 0, 0)
-    r = sum_rows(r)
-    r = lax.all_to_all(r, "zh", 0, 0)
+    r = lax.all_to_all(r.reshape((Y * ZH,) + r.shape[2:]), ("y", "zh"), 0, 0)
     r = spread_sum(r)
     r = lax.all_to_all(r, "y", 0, 0)
     r = spread_rows(r)

time: 321 us -> 311 us (0.969)
  the two profiles are of different devices: /device:TPU:10 before, /device:TPU:138 now
where the time goes in v2:
time: 311 us; the launch traced here: 310 us
  waiting for transfers between devices  137 us (44%)
  starting transfers between devices  113 us (36%)
  Pallas kernels  38.9 us (13%)
  blocking collectives  11.8 us (4%)
  local copies, waits for them, and re-layouts  6.3 us (2%)
    ppermute x4, waiting for transfers between devices, per_device(): lax.ppermute(part, 'zl', ring(ZL, k))  32.1 us
    ppermute x4, waiting for transfers between devices, per_device(): lax.ppermute(sends[k], ('zl', 'core', 'zh'), spread_pairs(k))  26.7 us
    ppermute x4, starting transfers between devices, per_device(): lax.ppermute(sends[k], ('zl', 'core', 'zh'), spread_pairs(k))  24.2 us
    ppermute x3, waiting for transfers between devices, per_device(): lax.ppermute(heads, 'x', ring(X, k))  21.6 us
    all_to_all x1, waiting for transfers between devices, per_device(): w_y = lax.all_to_all(w_y, 'y', 0, 0)  19.2 us
    ppermute x3, starting transfers between devices, per_device(): w_far = [lax.ppermute(w_part, 'zh', ring(ZH, k)) for k in range(1, ZH)]  17.9 us
    ppermute x3, waiting for transfers between devices, per_device(): lax.ppermute(part[k], 'x', ring(X, k))  16.4 us
    ppermute x3, waiting for transfers between devices, per_device(): w_far = [lax.ppermute(w_part, 'zh', ring(ZH, k)) for k in range(1, ZH)]  16.4 us
  transfers between devices with their start and end apart: 24, of which 17 were waited for; matrix products, arithmetic and copies ran while one was open for 1% of the time, Pallas kernels for 9%

profile of v2, /device:TPU:138, one launch (start us, length us, event | category | flops | bytes accessed | tf_op | source)
XLA Modules:
  0.0 309.9 jit_solution(2059336744128254092)
XLA Ops:
  2.0 12.2 %collective-permute-start.3 = (bf16[128,1024]{1,0:T(8,128)(2,1)S(1)}, bf16[128,1024]{1,0:T(8,128)(2,1)S(1)}, u32[]{:S(2)}, u32[]{:S(2)}) collective-permute-start(bf16[128,1024]{1,0:T(8,128)(2,1)S(1)} %get-tuple-element.18), channel_id=1, source_target_pairs={{0,12},{1,0},{2,4},{3,8},{4,5},{5,16},{6,20},{7,1},{8,21},{9,9},{1... | collective-permute-start | bytes 786440 | tf_op jit(solution)/shard_map/ppermute | solution.py:277
  20.1 6.1 %collective-permute-start.2 = (bf16[128,1024]{1,0:T(8,128)(2,1)S(1)}, bf16[128,1024]{1,0:T(8,128)(2,1)S(1)}, u32[]{:S(2)}, u32[]{:S(2)}) collective-permute-start(bf16[128,1024]{1,0:T(8,128)(2,1)S(1)} %get-tuple-element.21), channel_id=1, source_target_pairs={{0,8},{1,12},{2,0},{3,4},{4,1},{5,5},{6,16},{7,20},{8,17},{9,21},{... | collective-permute-start | bytes 786440 | tf_op jit(solution)/shard_map/ppermute | solution.py:277
  28.0 14.5 %collective-permute-done.1.refs_1_ = bf16[128,1024]{1,0:T(8,128)(2,1)S(1)} collective-permute-done((bf16[128,1024]{1,0:T(8,128)(2,1)S(1)}, bf16[128,1024]{1,0:T(8,128)(2,1)S(1)}, u32[]{:S(2)}, u32[]{:S(2)}) %collective-permute-start.1) | collective-permute-done | bytes 262176 | tf_op jit(solution)/shard_map/ppermute | solution.py:277
  42.6 10.3 %collective-permute-done.2.refs_2_ = bf16[128,1024]{1,0:T(8,128)(2,1)S(1)} collective-permute-done((bf16[128,1024]{1,0:T(8,128)(2,1)S(1)}, bf16[128,1024]{1,0:T(8,128)(2,1)S(1)}, u32[]{:S(2)}, u32[]{:S(2)}) %collective-permute-start.2) | collective-permute-done | bytes 262176 | tf_op jit(solution)/shard_map/ppermute | solution.py:277
  56.0 11.8 %all_to_all.30 = bf16[4,128,512]{2,1,0:T(8,128)(2,1)S(1)} all-to-all(bf16[4,128,512]{2,1,0:T(8,128)(2,1)} %get-tuple-element.10), channel_id=1, replica_groups=mesh['y'=8,'x'=4,'zl'=3,'core'=2,'zh'=4] {'x'}, dimensions={0} | all-to-all | bytes 1048576 | tf_op jit(solution)/shard_map/all_to_all | solution.py:285
  67.8 4.9 %all-to-all-start.1 = ((bf16[4,128,512]{2,1,0:T(8,128)(2,1)}), bf16[4,128,512]{2,1,0:T(8,128)(2,1)S(1)}, u32[]{:S(2)}, u32[]{:S(2)}) async-start(bf16[4,128,512]{2,1,0:T(8,128)(2,1)} %get-tuple-element.11), calls=%async_computation.1 | async-start | bytes 1048576 | tf_op jit(solution)/shard_map/all_to_all | solution.py:285
  90.3 11.4 %collective-permute-done.4 = bf16[512,512]{1,0:T(8,128)(2,1)} collective-permute-done((bf16[512,512]{1,0:T(8,128)(2,1)S(1)}, bf16[512,512]{1,0:T(8,128)(2,1)}, u32[]{:S(2)}, u32[]{:S(2)}) %collective-permute-start.4) | collective-permute-done | bytes 524320 | tf_op jit(solution)/shard_map/ppermute | solution.py:287
  104.8 8.0 %collective-permute-done.7 = bf16[512,512]{1,0:T(8,128)(2,1)S(1)} collective-permute-done((bf16[512,512]{1,0:T(8,128)(2,1)S(1)}, bf16[512,512]{1,0:T(8,128)(2,1)S(1)}, u32[]{:S(2)}, u32[]{:S(2)}) %collective-permute-start.7) | collective-permute-done | bytes 524320 | tf_op jit(solution)/shard_map/ppermute | solution.py:287
  112.8 8.6 %collective-permute-done.6 = bf16[512,512]{1,0:T(8,128)(2,1)S(1)} collective-permute-done((bf16[512,512]{1,0:T(8,128)(2,1)S(1)}, bf16[512,512]{1,0:T(8,128)(2,1)S(1)}, u32[]{:S(2)}, u32[]{:S(2)}) %collective-permute-start.6) | collective-permute-done | bytes 524320 | tf_op jit(solution)/shard_map/ppermute | solution.py:287
  135.0 9.5 %collective-permute-done.17.refs_2_ = bf16[768,384]{1,0:T(8,128)(2,1)} collective-permute-done((bf16[768,384]{1,0:T(8,128)(2,1)}, bf16[768,384]{1,0:T(8,128)(2,1)}, u32[]{:S(2)}, u32[]{:S(2)}) %collective-permute-start.17) | collective-permute-done | bytes 589856 | tf_op jit(solution)/shard_map/ppermute | solution.py:279
  144.5 12.2 %collective-permute-done.16.refs_1_ = bf16[768,384]{1,0:T(8,128)(2,1)} collective-permute-done((bf16[768,384]{1,0:T(8,128)(2,1)}, bf16[768,384]{1,0:T(8,128)(2,1)}, u32[]{:S(2)}, u32[]{:S(2)}) %collective-permute-start.16) | collective-permute-done | bytes 589856 | tf_op jit(solution)/shard_map/ppermute | solution.py:279
  165.0 5.0 %weight_part.3 = bf16[8,4,2,48,128]{4,3,2,1,0:T(8,128)(2,1)} custom-call(bf16[384,1536]{1,0:T(8,128)(2,1)} %get-tuple-element.16.a, bf16[384,1536]{1,0:T(8,128)(2,1)} %get-tuple-element.17.b, bf16[1536,512]{1,0:T(8,128)(2,1)} %copy-done.1, bf16[1536,512]{1,0:T(8,128)(2,1)} %collective-permute-done.9.refs_3_.d, bf16[8,4,48,128]{3,2,1,0:T(8,128)(2,1)} %weight_part.2.refs_0_), custom_call_target="tpu_custom_call" | custom-call | tf_op jit(solution)/shard_map/weight_part/pallas_call | solution.py:146
  170.0 10.9 %all-to-all-start.3 = ((bf16[32,2,48,128]{3,2,1,0:T(8,128)(2,1)}), bf16[32,2,48,128]{3,2,1,0:T(8,128)(2,1)S(1)}, u32[]{:S(2)}, u32[]{:S(2)}) async-start(bf16[32,2,48,128]{3,2,1,0:T(8,128)(2,1)} %bitcast.12), calls=%async_computation.3 | async-start | bytes 1572864 | tf_op jit(solution)/shard_map/all_to_all | solution.py:306
  181.7 6.4 %collective-permute-start.12 = (bf16[48,256]{1,0:T(8,128)(2,1)S(1)}, bf16[48,256]{1,0:T(8,128)(2,1)S(1)}, u32[]{:S(2)}, u32[]{:S(2)}) collective-permute-start(bf16[48,256]{1,0:T(8,128)(2,1)S(1)} %pad_maximum_fusion.2.refs_0_), channel_id=1, source_target_pairs={{0,3},{1,0},{2,1},{3,2},{4,7},{5,4},{6,5},{7,6},{8,11},{9,8},{10,9... | collective-permute-start | bytes 73736 | tf_op jit(solution)/shard_map/ppermute | solution.py:293
  188.1 5.8 %collective-permute-start.11 = (bf16[48,256]{1,0:T(8,128)(2,1)S(1)}, bf16[48,256]{1,0:T(8,128)(2,1)S(1)}, u32[]{:S(2)}, u32[]{:S(2)}) collective-permute-start(bf16[48,256]{1,0:T(8,128)(2,1)S(1)} %pad_maximum_fusion.2.refs_0_), channel_id=1, source_target_pairs={{0,2},{1,3},{2,0},{3,1},{4,6},{5,7},{6,4},{7,5},{8,10},{9,11},{10,... | collective-permute-start | bytes 73736 | tf_op jit(solution)/shard_map/ppermute | solution.py:293
  193.9 5.8 %collective-permute-start.10 = (bf16[48,256]{1,0:T(8,128)(2,1)S(1)}, bf16[48,256]{1,0:T(8,128)(2,1)S(1)}, u32[]{:S(2)}, u32[]{:S(2)}) collective-permute-start(bf16[48,256]{1,0:T(8,128)(2,1)S(1)} %pad_maximum_fusion.2.refs_0_), channel_id=1, source_target_pairs={{0,1},{1,2},{2,3},{3,0},{4,5},{5,6},{6,7},{7,4},{8,9},{9,10},{10,1... | collective-permute-start | bytes 73736 | tf_op jit(solution)/shard_map/ppermute | solution.py:293
  199.6 10.3 %collective-permute-done.12.refs_3_ = bf16[48,256]{1,0:T(8,128)(2,1)S(1)} collective-permute-done((bf16[48,256]{1,0:T(8,128)(2,1)S(1)}, bf16[48,256]{1,0:T(8,128)(2,1)S(1)}, u32[]{:S(2)}, u32[]{:S(2)}) %collective-permute-start.12) | collective-permute-done | bytes 24608 | tf_op jit(solution)/shard_map/ppermute | solution.py:293
  210.0 6.1 %collective-permute-done.11.refs_2_ = bf16[48,256]{1,0:T(8,128)(2,1)S(1)} collective-permute-done((bf16[48,256]{1,0:T(8,128)(2,1)S(1)}, bf16[48,256]{1,0:T(8,128)(2,1)S(1)}, u32[]{:S(2)}, u32[]{:S(2)}) %collective-permute-start.11) | collective-permute-done | bytes 24608 | tf_op jit(solution)/shard_map/ppermute | solution.py:293
  219.0 7.6 %all-to-all-start.2 = ((bf16[8,4,48,256]{3,2,1,0:T(8,128)(2,1)}), bf16[8,4,48,256]{3,2,1,0:T(8,128)(2,1)S(1)}, u32[]{:S(2)}, u32[]{:S(2)}) async-start(bf16[8,4,48,256]{3,2,1,0:T(8,128)(2,1)} %spread_cols.1), calls=%async_computation.2 | async-start | bytes 1572864 | tf_op jit(solution)/shard_map/all_to_all | solution.py:295
  228.5 19.2 %all-to-all-done.2.src = bf16[8,4,48,256]{3,2,1,0:T(8,128)(2,1)S(1)} async-done(((bf16[8,4,48,256]{3,2,1,0:T(8,128)(2,1)}), bf16[8,4,48,256]{3,2,1,0:T(8,128)(2,1)S(1)}, u32[]{:S(2)}, u32[]{:S(2)}) %all-to-all-start.2) | async-done | bytes 786464 | tf_op jit(solution)/shard_map/all_to_all | solution.py:295
  254.6 9.4 %heads_part.1 = (bf16[768,384]{1,0:T(8,128)(2,1)}, bf16[768,384]{1,0:T(8,128)(2,1)}, bf16[768,384]{1,0:T(8,128)(2,1)}, bf16[768,384]{1,0:T(8,128)(2,1)}) custom-call(s32[1]{0:T(128)} %bitcast.at_ref, s32[6]{0:T(128)} %stack.34.rows_ref, bf16[1536,512]{1,0:T(8,128)(2,1)} %copy-done, bf16[1536,512]{1,0:T(8,128)(2,1)} %copy-done.1, ...), custom_call_target="tpu_custom_call" | custom-call | tf_op jit(solution)/shard_map/heads_part/pallas_call | solution.py:179
  276.9 5.0 %all-to-all-start.5 = ((bf16[4,2,384,128]{3,2,1,0:T(8,128)(2,1)}), bf16[4,2,384,128]{3,2,1,0:T(8,128)(2,1)S(1)}, u32[]{:S(2)}, u32[]{:S(2)}) async-start(bf16[4,2,384,128]{3,2,1,0:T(8,128)(2,1)} %spread_rows.1), calls=%async_computation.5 | async-start | bytes 1572864 | tf_op jit(solution)/shard_map/all_to_all | solution.py:310
  282.3 4.9 %collective-permute-done.14.refs_2_ = bf16[768,384]{1,0:T(8,128)(2,1)S(1)} collective-permute-done((bf16[768,384]{1,0:T(8,128)(2,1)}, bf16[768,384]{1,0:T(8,128)(2,1)S(1)}, u32[]{:S(2)}, u32[]{:S(2)}) %collective-permute-start.14) | collective-permute-done | bytes 589856 | tf_op jit(solution)/shard_map/ppermute | solution.py:314
  287.2 11.2 %collective-permute-done.15.refs_3_ = bf16[768,384]{1,0:T(8,128)(2,1)S(1)} collective-permute-done((bf16[768,384]{1,0:T(8,128)(2,1)}, bf16[768,384]{1,0:T(8,128)(2,1)S(1)}, u32[]{:S(2)}, u32[]{:S(2)}) %collective-permute-start.15) | collective-permute-done | bytes 589856 | tf_op jit(solution)/shard_map/ppermute | solution.py:314
  (78 shorter events, 91.9 us)
Async XLA Ops:
  2.0 26.1 %collective-permute-start.3 = (bf16[128,1024]{1,0:T(8,128)(2,1)S(1)}, bf16[128,1024]{1,0:T(8,128)(2,1)S(1)}, u32[]{:S(2)}, u32[]{:S(2)}) collective-permute-start(bf16[128,1024]{1,0:T(8,128)(2,1)S(1)} %get-tuple-element.18), channel_id=1, source_target_pairs={{0,12},{1,0},{2,4},{3,8},{4,5},{5,16},{6,20},{7,1},{8,21},{9,9},{1... | collective-permute-start | bytes 786440 | tf_op jit(solution)/shard_map/ppermute | solution.py:277
  14.2 28.4 %collective-permute-start.1 = (bf16[128,1024]{1,0:T(8,128)(2,1)S(1)}, bf16[128,1024]{1,0:T(8,128)(2,1)S(1)}, u32[]{:S(2)}, u32[]{:S(2)}) collective-permute-start(bf16[128,1024]{1,0:T(8,128)(2,1)S(1)} %get-tuple-element.19), channel_id=1, source_target_pairs={{0,4},{1,8},{2,12},{3,0},{4,20},{5,1},{6,5},{7,16},{8,13},{9,17},{... | collective-permute-start | bytes 786440 | tf_op jit(solution)/shard_map/ppermute | solution.py:277
  18.2 24.4 %collective-permute-start = (bf16[128,1024]{1,0:T(8,128)(2,1)S(1)}, bf16[128,1024]{1,0:T(8,128)(2,1)S(1)}, u32[]{:S(2)}, u32[]{:S(2)}) collective-permute-start(bf16[128,1024]{1,0:T(8,128)(2,1)S(1)} %get-tuple-element.20), channel_id=1, source_target_pairs={{0,0},{1,4},{2,8},{3,12},{4,16},{5,20},{6,1},{7,5},{8,9},{9,13},{1... | collective-permute-start | bytes 786440 | tf_op jit(solution)/shard_map/ppermute | solution.py:277
  20.1 32.8 %collective-permute-start.2 = (bf16[128,1024]{1,0:T(8,128)(2,1)S(1)}, bf16[128,1024]{1,0:T(8,128)(2,1)S(1)}, u32[]{:S(2)}, u32[]{:S(2)}) collective-permute-start(bf16[128,1024]{1,0:T(8,128)(2,1)S(1)} %get-tuple-element.21), channel_id=1, source_target_pairs={{0,8},{1,12},{2,0},{3,4},{4,1},{5,5},{6,16},{7,20},{8,17},{9,21},{... | collective-permute-start | bytes 786440 | tf_op jit(solution)/shard_map/ppermute | solution.py:277
  67.8 11.6 %all-to-all-start.1 = ((bf16[4,128,512]{2,1,0:T(8,128)(2,1)}), bf16[4,128,512]{2,1,0:T(8,128)(2,1)S(1)}, u32[]{:S(2)}, u32[]{:S(2)}) async-start(bf16[4,128,512]{2,1,0:T(8,128)(2,1)} %get-tuple-element.11), calls=%async_computation.1 | async-start | bytes 1048576 | tf_op jit(solution)/shard_map/all_to_all | solution.py:285
  72.7 17.6 %collective-permute-start.5 = (bf16[512,512]{1,0:T(8,128)(2,1)S(1)}, bf16[512,512]{1,0:T(8,128)(2,1)S(1)}, u32[]{:S(2)}, u32[]{:S(2)}) collective-permute-start(bf16[512,512]{1,0:T(8,128)(2,1)S(1)} %bitcast.16), channel_id=1, source_target_pairs={{0,16},{8,0},{16,8},{1,17},{9,1},{17,9},{2,18},{10,2},{18,10},{3,1... | collective-permute-start | bytes 1572872 | tf_op jit(solution)/shard_map/ppermute | solution.py:287
  76.2 25.5 %collective-permute-start.4 = (bf16[512,512]{1,0:T(8,128)(2,1)S(1)}, bf16[512,512]{1,0:T(8,128)(2,1)}, u32[]{:S(2)}, u32[]{:S(2)}) collective-permute-start(bf16[512,512]{1,0:T(8,128)(2,1)S(1)} %bitcast.17), channel_id=1, source_target_pairs={{0,8},{8,16},{16,0},{1,9},{9,17},{17,1},{2,10},{10,18},{18,2},{3,1... | collective-permute-start | bytes 1572872 | tf_op jit(solution)/shard_map/ppermute | solution.py:287
  79.5 33.4 %collective-permute-start.7 = (bf16[512,512]{1,0:T(8,128)(2,1)S(1)}, bf16[512,512]{1,0:T(8,128)(2,1)S(1)}, u32[]{:S(2)}, u32[]{:S(2)}) collective-permute-start(bf16[512,512]{1,0:T(8,128)(2,1)S(1)} %bitcast.13), channel_id=1, source_target_pairs={{0,16},{8,0},{16,8},{1,17},{9,1},{17,9},{2,18},{10,2},{18,10},{3,1... | collective-permute-start | bytes 1572872 | tf_op jit(solution)/shard_map/ppermute | solution.py:287
  83.8 37.6 %collective-permute-start.6 = (bf16[512,512]{1,0:T(8,128)(2,1)S(1)}, bf16[512,512]{1,0:T(8,128)(2,1)S(1)}, u32[]{:S(2)}, u32[]{:S(2)}) collective-permute-start(bf16[512,512]{1,0:T(8,128)(2,1)S(1)} %bitcast.14), channel_id=1, source_target_pairs={{0,8},{8,16},{16,0},{1,9},{9,17},{17,1},{2,10},{10,18},{18,2},{3,1... | collective-permute-start | bytes 1572872 | tf_op jit(solution)/shard_map/ppermute | solution.py:287
  102.9 57.4 %collective-permute-start.8 = (bf16[1536,512]{1,0:T(8,128)(2,1)S(1)}, bf16[1536,512]{1,0:T(8,128)(2,1)}, u32[]{:S(2)}, u32[]{:S(2)}) collective-permute-start(bf16[1536,512]{1,0:T(8,128)(2,1)S(1)} %pad_maximum_fusion.refs_0_.c), channel_id=1, source_target_pairs={{0,4},{4,0},{1,5},{5,1},{2,6},{6,2},{3,7},{7,3},{8,12},{12,8},{9,1... | collective-permute-start | bytes 4718600 | tf_op jit(solution)/shard_map/ppermute | solution.py:301
  122.6 42.4 %collective-permute-start.9 = (bf16[1536,512]{1,0:T(8,128)(2,1)S(1)}, bf16[1536,512]{1,0:T(8,128)(2,1)}, u32[]{:S(2)}, u32[]{:S(2)}) collective-permute-start(bf16[1536,512]{1,0:T(8,128)(2,1)S(1)} %pad_maximum_fusion.1.refs_1_.c), channel_id=1, source_target_pairs={{0,4},{4,0},{1,5},{5,1},{2,6},{6,2},{3,7},{7,3},{8,12},{12,8},{9,1... | collective-permute-start | bytes 4718600 | tf_op jit(solution)/shard_map/ppermute | solution.py:301
  124.5 20.0 %collective-permute-start.17 = (bf16[768,384]{1,0:T(8,128)(2,1)}, bf16[768,384]{1,0:T(8,128)(2,1)}, u32[]{:S(2)}, u32[]{:S(2)}) collective-permute-start(bf16[768,384]{1,0:T(8,128)(2,1)} %refs_0_.1), channel_id=1, source_target_pairs={{0,48},{24,72},{48,0},{72,24},{1,49},{25,73},{49,1},{73,25},{2,50}... | collective-permute-start | bytes 1769480 | tf_op jit(solution)/shard_map/ppermute | solution.py:279
  128.5 28.1 %collective-permute-start.16 = (bf16[768,384]{1,0:T(8,128)(2,1)}, bf16[768,384]{1,0:T(8,128)(2,1)}, u32[]{:S(2)}, u32[]{:S(2)}) collective-permute-start(bf16[768,384]{1,0:T(8,128)(2,1)} %refs_0_.1), channel_id=1, source_target_pairs={{0,24},{24,48},{48,72},{72,0},{1,25},{25,49},{49,73},{73,1},{2,26}... | collective-permute-start | bytes 1769480 | tf_op jit(solution)/shard_map/ppermute | solution.py:279
  130.5 26.2 %collective-permute-start.18 = (bf16[768,384]{1,0:T(8,128)(2,1)}, bf16[768,384]{1,0:T(8,128)(2,1)}, u32[]{:S(2)}, u32[]{:S(2)}) collective-permute-start(bf16[768,384]{1,0:T(8,128)(2,1)} %refs_0_.1), channel_id=1, source_target_pairs={{0,72},{24,0},{48,24},{72,48},{1,73},{25,1},{49,25},{73,49},{2,74}... | collective-permute-start | bytes 1769480 | tf_op jit(solution)/shard_map/ppermute | solution.py:279
  170.0 49.0 %all-to-all-start.3 = ((bf16[32,2,48,128]{3,2,1,0:T(8,128)(2,1)}), bf16[32,2,48,128]{3,2,1,0:T(8,128)(2,1)S(1)}, u32[]{:S(2)}, u32[]{:S(2)}) async-start(bf16[32,2,48,128]{3,2,1,0:T(8,128)(2,1)} %bitcast.12), calls=%async_computation.3 | async-start | bytes 1572864 | tf_op jit(solution)/shard_map/all_to_all | solution.py:306
  181.7 28.3 %collective-permute-start.12 = (bf16[48,256]{1,0:T(8,128)(2,1)S(1)}, bf16[48,256]{1,0:T(8,128)(2,1)S(1)}, u32[]{:S(2)}, u32[]{:S(2)}) collective-permute-start(bf16[48,256]{1,0:T(8,128)(2,1)S(1)} %pad_maximum_fusion.2.refs_0_), channel_id=1, source_target_pairs={{0,3},{1,0},{2,1},{3,2},{4,7},{5,4},{6,5},{7,6},{8,11},{9,8},{10,9... | collective-permute-start | bytes 73736 | tf_op jit(solution)/shard_map/ppermute | solution.py:293
  188.1 28.0 %collective-permute-start.11 = (bf16[48,256]{1,0:T(8,128)(2,1)S(1)}, bf16[48,256]{1,0:T(8,128)(2,1)S(1)}, u32[]{:S(2)}, u32[]{:S(2)}) collective-permute-start(bf16[48,256]{1,0:T(8,128)(2,1)S(1)} %pad_maximum_fusion.2.refs_0_), channel_id=1, source_target_pairs={{0,2},{1,3},{2,0},{3,1},{4,6},{5,7},{6,4},{7,5},{8,10},{9,11},{10,... | collective-permute-start | bytes 73736 | tf_op jit(solution)/shard_map/ppermute | solution.py:293
  193.9 22.2 %collective-permute-start.10 = (bf16[48,256]{1,0:T(8,128)(2,1)S(1)}, bf16[48,256]{1,0:T(8,128)(2,1)S(1)}, u32[]{:S(2)}, u32[]{:S(2)}) collective-permute-start(bf16[48,256]{1,0:T(8,128)(2,1)S(1)} %pad_maximum_fusion.2.refs_0_), channel_id=1, source_target_pairs={{0,1},{1,2},{2,3},{3,0},{4,5},{5,6},{6,7},{7,4},{8,9},{9,10},{10,1... | collective-permute-start | bytes 73736 | tf_op jit(solution)/shard_map/ppermute | solution.py:293
  219.0 28.7 %all-to-all-start.2 = ((bf16[8,4,48,256]{3,2,1,0:T(8,128)(2,1)}), bf16[8,4,48,256]{3,2,1,0:T(8,128)(2,1)S(1)}, u32[]{:S(2)}, u32[]{:S(2)}) async-start(bf16[8,4,48,256]{3,2,1,0:T(8,128)(2,1)} %spread_cols.1), calls=%async_computation.2 | async-start | bytes 1572864 | tf_op jit(solution)/shard_map/all_to_all | solution.py:295
  247.7 26.7 %all-to-all-start.4 = ((bf16[8,2,48,128]{3,2,1,0:T(8,128)(2,1)}), bf16[8,2,48,128]{3,2,1,0:T(8,128)(2,1)S(1)}, u32[]{:S(2)}, u32[]{:S(2)}) async-start(bf16[8,2,48,128]{3,2,1,0:T(8,128)(2,1)} %spread_sum.1), calls=%async_computation.4 | async-start | bytes 393216 | tf_op jit(solution)/shard_map/all_to_all | solution.py:308
  264.0 18.3 %collective-permute-start.13 = (bf16[768,384]{1,0:T(8,128)(2,1)}, bf16[768,384]{1,0:T(8,128)(2,1)S(1)}, u32[]{:S(2)}, u32[]{:S(2)}) collective-permute-start(bf16[768,384]{1,0:T(8,128)(2,1)} %get-tuple-element.13), channel_id=1, source_target_pairs={{0,24},{24,48},{48,72},{72,0},{1,25},{25,49},{49,73},{73,1},{2,26}... | collective-permute-start | bytes 1769480 | tf_op jit(solution)/shard_map/ppermute | solution.py:314
  267.3 19.9 %collective-permute-start.14 = (bf16[768,384]{1,0:T(8,128)(2,1)}, bf16[768,384]{1,0:T(8,128)(2,1)S(1)}, u32[]{:S(2)}, u32[]{:S(2)}) collective-permute-start(bf16[768,384]{1,0:T(8,128)(2,1)} %get-tuple-element.14), channel_id=1, source_target_pairs={{0,48},{24,72},{48,0},{72,24},{1,49},{25,73},{49,1},{73,25},{2,50}... | collective-permute-start | bytes 1769480 | tf_op jit(solution)/shard_map/ppermute | solution.py:314
  270.0 28.4 %collective-permute-start.15 = (bf16[768,384]{1,0:T(8,128)(2,1)}, bf16[768,384]{1,0:T(8,128)(2,1)S(1)}, u32[]{:S(2)}, u32[]{:S(2)}) collective-permute-start(bf16[768,384]{1,0:T(8,128)(2,1)} %get-tuple-element.15), channel_id=1, source_target_pairs={{0,72},{24,0},{48,24},{72,48},{1,73},{25,1},{49,25},{73,49},{2,74}... | collective-permute-start | bytes 1769480 | tf_op jit(solution)/shard_map/ppermute | solution.py:314
  276.9 29.8 %all-to-all-start.5 = ((bf16[4,2,384,128]{3,2,1,0:T(8,128)(2,1)}), bf16[4,2,384,128]{3,2,1,0:T(8,128)(2,1)S(1)}, u32[]{:S(2)}, u32[]{:S(2)}) async-start(bf16[4,2,384,128]{3,2,1,0:T(8,128)(2,1)} %spread_rows.1), calls=%async_computation.5 | async-start | bytes 1572864 | tf_op jit(solution)/shard_map/all_to_all | solution.py:310
  (18 other events, 215.4 us)
